TPU v7x, 512 devices: a whole 4x4x16 slice. The times are simulated.
512 devices in a mesh: dp: 64 (over y, z), expert: 8 (over x, core).
Axes of the slice: x: 4, y: 4, z: 16, core: 2. Of those that a mesh axis runs over, the one named last changes fastest.
Arguments:
- tokens: bfloat16 [32768, 2048], P(('dp', 'expert')), may hold values from -16 to 16
- cotangent: bfloat16 [32768, 2048], P(('dp', 'expert')), may hold values from -8 to 8
- route: int32 [65536], P(('dp', 'expert')), may hold values from 0 to 63, as said below
- counts: int32 [512, 8], P(('dp', 'expert')), may hold values from 8 to 16, as said below
- gate_master: float32 [8, 2048, 768], P('expert', 'dp'), may hold values from -0.125 to 0.125
- up_master: float32 [8, 2048, 768], P('expert', 'dp'), may hold values from -0.125 to 0.125
- down_master: float32 [8, 2048, 768], P('expert', 'dp'), may hold values from -0.21875 to 0.21875
- first_moment: float32 [8, 3, 2048, 768], P('expert', None, 'dp'), may hold values from -2 to 2
- second_moment: float32 [8, 3, 2048, 768], P('expert', None, 'dp'), may hold values from 0.01 to 1
Outputs:
- combined: float32 [8, 3, 2048, 768], P('expert', None, 'dp')
- new_weights: float32 [8, 3, 2048, 768], P('expert', None, 'dp')
- new_first: float32 [8, 3, 2048, 768], P('expert', None, 'dp')
- new_second: float32 [8, 3, 2048, 768], P('expert', None, 'dp')
- forward: bfloat16 [32768, 2048], P(('dp', 'expert'))
Inputs may be any that keep to these rules, and one draw needn't show every extreme that they name: `route`: for each device and each expert, the 16 slots name distinct local token rows. `counts`: in every draw, for some data index and some expert, every source device of that data index sends exactly 16 live slots.
All inputs are finite; a program needn't handle non-finite values.
Results may differ from a plain program's by a relative error of at most 0.011.
The roundings to bfloat16 on the way count: a program that leaves them out, or rounds other values in their place, can miss the bound.
Values may be sent and summed in bfloat16 or wider, within the bound.
A program may use at most 128 MiB of HBM per device.

v0:
```python
import jax
import jax.numpy as jnp
from jax import lax
from jax.sharding import Mesh
from jax.sharding import PartitionSpec as P

DP = ("dp_0", "dp_1")
EXPERT = ("expert_0", "expert_1")
DP_EXPERT = ("dp_0", "dp_1", "expert_0", "expert_1")


first_decay = 0.9
second_decay = 0.95
learn_rate = 0.01
adam_eps = 1e-08
weight_decay = 0.1
adam_count = 100.0
norm_eps = 1e-06
contract_rows = (((0,), (0,)), ((), ()))
contract_last = (((1,), (1,)), ((), ()))


def swapped(array, axis, apart):
    return lax.ppermute(array, axis, [(i, i ^ 1 << apart) for i in range(lax.axis_size(axis))])


def joined_along(parts, dim):
    shape = list(parts.shape[1:])
    shape[dim] *= parts.shape[0]
    return jnp.moveaxis(parts, 0, dim).reshape(shape)


def all_blocks(array, axes, turns):
    parts = array[None]
    for k in turns:
        parts = lax.all_gather(parts, axes[k], axis=0, tiled=True)
    current = [lax.axis_size(axes[k]) for k in reversed(turns)]
    parts = parts.reshape(*current, *array.shape)
    turned = sorted(range(len(turns)), key=lambda place: turns[len(turns) - 1 - place])
    return parts.transpose(*turned, *range(len(turns), parts.ndim)).reshape(-1, *array.shape)


def gather_axes(array, axes, turns, dim):
    return joined_along(all_blocks(array, axes, turns), dim)


def split_up(array, dim, size):
    shape = array.shape
    parts = array.reshape(*shape[:dim], size, shape[dim] // size, *shape[dim + 1 :])
    return jnp.moveaxis(parts, dim, 0)


def turned_blocks(parts, axes, turns):
    inside = parts.shape[1:]
    out = parts.reshape(*(lax.axis_size(a) for a in axes), *inside)
    for k in turns:
        out = lax.all_to_all(out, axes[k], k, k, tiled=True)
    return out.reshape(-1, *inside)


def exchange_by_axis(array, axes, turns, split_dim, concat_dim):
    parts = split_up(array, split_dim, lax.axis_size(axes))
    return joined_along(turned_blocks(parts, axes, turns), concat_dim)


def weight_grads(token_cols, grad_cols, d_gate, d_up, hidden_act):
    return jnp.stack(
        [
            lax.dot_general(token_cols, d_gate, contract_rows, preferred_element_type=jnp.float32),
            lax.dot_general(token_cols, d_up, contract_rows, preferred_element_type=jnp.float32),
            lax.dot_general(
                grad_cols, hidden_act, contract_rows, preferred_element_type=jnp.float32
            ),
        ]
    )


def half_columns(matrix, dp_parts, selected):
    shaped = matrix.reshape(matrix.shape[0], dp_parts // 2, 2, matrix.shape[1] // dp_parts)
    chosen = lax.dynamic_index_in_dim(shaped, selected, 2, keepdims=False)
    return chosen.reshape(matrix.shape[0], matrix.shape[1] // 2)


def group_sum(partial_value, level_index):
    total = partial_value
    for bit_index in range(level_index + 1):
        total = total + swapped(total, DP, bit_index)
    return total


def combine_level(kept_half, received_half, own_bit, level_index):
    mine_wide = kept_half.astype(jnp.float32)
    theirs_wide = received_half.astype(jnp.float32)
    cross = jnp.sum(mine_wide * theirs_wide, axis=(1, 2, 3))
    own_square = jnp.sum(mine_wide * mine_wide, axis=(1, 2, 3))
    their_square = jnp.sum(theirs_wide * theirs_wide, axis=(1, 2, 3))
    is_lower = own_bit == 0
    lower_square = jnp.where(is_lower, own_square, their_square)
    upper_square = jnp.where(is_lower, their_square, own_square)
    totals = group_sum(jnp.stack([cross, lower_square, upper_square]), level_index)
    lower_coef = 1.0 - totals[0] / (2.0 * (totals[1] + norm_eps))
    upper_coef = 1.0 - totals[0] / (2.0 * (totals[2] + norm_eps))
    own_coef = jnp.where(is_lower, lower_coef, upper_coef)
    their_coef = jnp.where(is_lower, upper_coef, lower_coef)
    return own_coef[:, None, None, None] * mine_wide + their_coef[:, None, None, None] * theirs_wide


def shards(
    tokens,
    cotangent,
    route,
    counts,
    gate_master,
    up_master,
    down_master,
    first_moment,
    second_moment,
):
    experts = lax.axis_size(EXPERT)
    dp_parts = lax.axis_size(DP)
    levels = dp_parts.bit_length() - 1
    my_index = lax.axis_index(DP)
    slot_count = route.shape[0]
    capacity = slot_count // experts
    slot_ids = jnp.arange(slot_count, dtype=jnp.int32)
    live_slots = slot_ids % capacity < jnp.repeat(counts[0], capacity)
    sent_tokens = jnp.where(live_slots[:, None], jnp.take(tokens, route, axis=0), 0)
    sent_grads = jnp.where(live_slots[:, None], jnp.take(cotangent, route, axis=0), 0)
    token_rows, grad_rows = (
        lax.all_to_all(sent_tokens, EXPERT, split_axis=0, concat_axis=0, tiled=True),
        lax.all_to_all(sent_grads, EXPERT, split_axis=0, concat_axis=0, tiled=True),
    )
    masters = jnp.stack([gate_master[0], up_master[0], down_master[0]])
    compute_weights = masters.astype(jnp.bfloat16)
    block_rows = masters.shape[1]
    hidden_width = masters.shape[2]
    full_weights = gather_axes(compute_weights, DP, (0, 1), 1)
    gate_pre = jnp.dot(token_rows, full_weights[0], preferred_element_type=jnp.float32)
    up_pre = jnp.dot(token_rows, full_weights[1], preferred_element_type=jnp.float32)
    back_hidden = jnp.dot(grad_rows, full_weights[2], preferred_element_type=jnp.float32)
    sigmoid_gate = jax.nn.sigmoid(gate_pre)
    active_gate = gate_pre * sigmoid_gate
    hidden_act = (active_gate * up_pre).astype(jnp.bfloat16)
    d_gate = (back_hidden * up_pre * sigmoid_gate * (1.0 + gate_pre * (1.0 - sigmoid_gate))).astype(
        jnp.bfloat16
    )
    d_up = (back_hidden * active_gate).astype(jnp.bfloat16)
    low_bit = my_index & 1
    shape_half = (3, dp_parts // 2, block_rows, hidden_width)
    held_blocks = None
    give_tokens = half_columns(token_rows, dp_parts, 1 - low_bit)
    give_grads = half_columns(grad_rows, dp_parts, 1 - low_bit)
    got_tokens, got_grads, got_dgate, got_dup, got_hidden = swapped(
        (give_tokens, give_grads, d_gate, d_up, hidden_act), DP, 0
    )
    part_grads = weight_grads(
        half_columns(token_rows, dp_parts, low_bit),
        half_columns(grad_rows, dp_parts, low_bit),
        d_gate,
        d_up,
        hidden_act,
    )
    own_part = part_grads.astype(jnp.bfloat16).reshape(shape_half)
    their_part = (
        weight_grads(got_tokens, got_grads, got_dgate, got_dup, got_hidden)
        .astype(jnp.bfloat16)
        .reshape(shape_half)
    )
    wide_blocks = combine_level(own_part, their_part, low_bit, 0)
    held_blocks = wide_blocks.astype(jnp.bfloat16)
    first_level = 1
    for level_index in range(first_level, levels):
        own_bit = my_index >> level_index & 1
        grouped = held_blocks.reshape(3, held_blocks.shape[1] // 2, 2, block_rows, hidden_width)
        kept_half = lax.dynamic_index_in_dim(grouped, own_bit, 2, keepdims=False)
        given_half = lax.dynamic_index_in_dim(grouped, 1 - own_bit, 2, keepdims=False)
        received_half = swapped(given_half, DP, level_index)
        wide_blocks = combine_level(kept_half, received_half, own_bit, level_index)
        held_blocks = wide_blocks if level_index + 1 == levels else wide_blocks.astype(jnp.bfloat16)
    combined = held_blocks[:, 0]
    new_first = first_decay * first_moment[0] + (1.0 - first_decay) * combined
    new_second = second_decay * second_moment[0] + (1.0 - second_decay) * combined * combined
    first_hat = new_first / (1.0 - first_decay**adam_count)
    second_hat = new_second / (1.0 - second_decay**adam_count)
    new_masters = masters - learn_rate * (
        first_hat / (jnp.sqrt(second_hat) + adam_eps) + weight_decay * masters
    )
    new_down = new_masters[2].astype(jnp.bfloat16)
    full_down = gather_axes(new_down, DP, (0, 1), 0)
    slot_outputs = lax.dot_general(
        hidden_act, full_down, contract_last, preferred_element_type=jnp.float32
    ).astype(jnp.bfloat16)
    returned = exchange_by_axis(slot_outputs, EXPERT, (1, 0), 0, 0)
    pool_ids = jnp.arange(tokens.shape[0], dtype=jnp.int32)
    selector = ((route[None, :] == pool_ids[:, None]) & live_slots[None, :]).astype(jnp.bfloat16)
    forward = jnp.dot(selector, returned, preferred_element_type=jnp.float32).astype(jnp.bfloat16)
    return (combined[None], new_masters[None], new_first[None], new_second[None], forward)


def solution(mesh):
    split = Mesh(mesh.devices.reshape(4, 16, 4, 2), ("dp_0", "dp_1", "expert_0", "expert_1"))
    return jax.shard_map(
        shards,
        mesh=split,
        in_specs=(
            P(DP_EXPERT, None),
            P(DP_EXPERT, None),
            P(DP_EXPERT),
            P(DP_EXPERT, None),
            P(EXPERT, DP, None),
            P(EXPERT, DP, None),
            P(EXPERT, DP, None),
            P(EXPERT, None, DP, None),
            P(EXPERT, None, DP, None),
        ),
        out_specs=(
            P(EXPERT, None, DP, None),
            P(EXPERT, None, DP, None),
            P(EXPERT, None, DP, None),
            P(EXPERT, None, DP, None),
            P(DP_EXPERT, None),
        ),
        check_vma=False,
    )
```

profile of v0, /device:TPU:7, one launch (start us, length us, event | category | flops | bytes accessed | tf_op | source)
XLA Modules:
  0.0 777.5 jit_solution(9682907072181180259)
XLA Ops:
  8.3 12.4 %all_gather.12 = bf16[4,3,32,768]{3,2,1,0:T(8,128)(2,1)} all-gather(bf16[1,3,32,768]{3,2,1,0:T(8,128)(2,1)S(1)} %fusion.33), channel_id=1, replica_groups=mesh['dp_0'=4,'dp_1'=16,'expert_0'=4,'expert_1'=2] {'dp_0'}, dimensions={0}, use_global_device_ids=true | all-gather | bytes 737280 | tf_op jit(solution)/shard_map/all_gather | solution.py:36
  25.2 17.8 %all_to_all.34 = bf16[8,16,2048]{2,1,0:T(8,128)(2,1)S(1)} all-to-all(bf16[8,16,2048]{2,1,0:T(8,128)(2,1)S(1)} %bitcast.191), channel_id=1, replica_groups=mesh['dp_0'=4,'dp_1'=16,'expert_0'=4,'expert_1'=2] {'expert_0','expert_1'}, dimensions={0} | all-to-all | bytes 1048576 | tf_op jit(solution)/shard_map/all_to_all | solution.py:131
  43.0 6.2 all-to-all-start
  50.8 7.4 constant_dynamic-slice_fusion.3
  58.2 5.4 copy.55
  63.6 3.3 copy.57
  70.6 7.4 constant_dynamic-slice_fusion.4
  78.1 4.8 copy.53
  82.9 3.3 copy.56
  86.2 3.3 collective-permute-start
  89.6 62.5 %all-gather.3.cloned.1.call-done = bf16[64,3,32,768]{3,2,1,0:T(8,128)(2,1)} async-done(((bf16[4,3,32,768]{3,2,1,0:T(8,128)(2,1)}), bf16[64,3,32,768]{3,2,1,0:T(8,128)(2,1)}) %all-gather.3.cloned.1.call-update) | async-done | bytes 9437200 | tf_op jit(solution)/shard_map/all_gather | solution.py:36
  152.1 8.5 %copy.54 = bf16[4,16,3,32,768]{4,3,2,1,0:T(8,128)(2,1)} copy(bf16[4,16,3,32,768]{4,3,2,0,1:T(8,128)(2,1)} %bitcast.176) | data formatting | bytes 18874368 | tf_op jit(solution)/shard_map/transpose | solution.py:40
  160.6 4.1 fusion.101
  166.8 2.7 collective-permute-start.1
  169.5 2.7 collective-permute-start.2
  173.3 2.8 collective-permute-start.4
  179.4 3.1 collective-permute-done.4
  184.0 3.7 fusion.1
  187.8 2.7 collective-permute-start.5
  192.1 2.2 add_convert_fusion
  197.2 4.5 collective-permute-start.6
  201.7 102.2 %collective-permute-done.6 = bf16[3,16,32,768]{3,2,1,0:T(8,128)(2,1)S(1)} collective-permute-done((bf16[3,16,32,768]{3,2,1,0:T(8,128)(2,1)}, bf16[3,16,32,768]{3,2,1,0:T(8,128)(2,1)S(1)}, u32[]{:S(2)}, u32[]{:S(2)}) %collective-permute-start.6) | collective-permute-done | bytes 2359328 | tf_op jit(solution)/shard_map/ppermute | solution.py:24
  303.9 4.2 fusion.6
  310.0 2.4 collective-permute-done.7
  312.5 2.8 collective-permute-start.8
  315.3 2.4 collective-permute-done.8
  317.7 2.7 fusion.5
  321.6 7.5 collective-permute-start.9
  329.1 102.3 %collective-permute-done.9 = bf16[3,8,32,768]{3,2,1,0:T(8,128)(2,1)} collective-permute-done((bf16[3,8,32,768]{3,2,1,0:T(8,128)(2,1)}, bf16[3,8,32,768]{3,2,1,0:T(8,128)(2,1)}, u32[]{:S(2)}, u32[]{:S(2)}) %collective-permute-start.9) | collective-permute-done | bytes 1179680 | tf_op jit(solution)/shard_map/ppermute | solution.py:24
  435.5 2.4 collective-permute-done.10
  439.8 3.3 collective-permute-done.11
  443.1 5.7 collective-permute-start.12
  448.8 2.6 collective-permute-done.12
  454.3 11.1 %collective-permute-start.13 = (bf16[3,4,32,768]{3,2,1,0:T(8,128)(2,1)S(1)}, bf16[3,4,32,768]{3,2,1,0:T(8,128)(2,1)S(1)}, u32[]{:S(2)}, u32[]{:S(2)}) collective-permute-start(bf16[3,4,32,768]{3,2,1,0:T(8,128)(2,1)S(1)} %dynamic-slice_bitcast_fusion.2), channel_id=1, source_target_pairs={{0,64},{8,72},{16,80},{24,88},{32,96},{40,104},{48,112},{56,120},{... | collective-permute-start | bytes 1769480 | tf_op jit(solution)/shard_map/ppermute | solution.py:24
  465.4 33.4 %collective-permute-done.13 = bf16[3,4,32,768]{3,2,1,0:T(8,128)(2,1)S(1)} collective-permute-done((bf16[3,4,32,768]{3,2,1,0:T(8,128)(2,1)S(1)}, bf16[3,4,32,768]{3,2,1,0:T(8,128)(2,1)S(1)}, u32[]{:S(2)}, u32[]{:S(2)}) %collective-permute-start.13) | collective-permute-done | bytes 589856 | tf_op jit(solution)/shard_map/ppermute | solution.py:24
  500.3 13.0 %collective-permute-start.14 = (f32[3,3]{1,0:T(4,128)S(1)}, f32[3,3]{1,0:T(4,128)S(1)}, u32[]{:S(2)}, u32[]{:S(2)}) collective-permute-start(f32[3,3]{1,0:T(4,128)S(1)} %pad_maximum_fusion.8), channel_id=1, source_target_pairs={{0,8},{8,0},{16,24},{24,16},{32,40},{40,32},{48,56},{56,48},{64,72... | collective-permute-start | bytes 116 | tf_op jit(solution)/shard_map/ppermute | solution.py:24
  514.3 2.7 collective-permute-start.15
  517.0 2.6 collective-permute-done.15
  519.6 15.2 %collective-permute-start.16 = (f32[3,3]{1,0:T(4,128)S(1)}, f32[3,3]{1,0:T(4,128)S(1)}, u32[]{:S(2)}, u32[]{:S(2)}) collective-permute-start(f32[3,3]{1,0:T(4,128)S(1)} %fusion.127), channel_id=1, source_target_pairs={{0,32},{8,40},{16,48},{24,56},{32,0},{40,8},{48,16},{56,24},{64,96... | collective-permute-start | bytes 116 | tf_op jit(solution)/shard_map/ppermute | solution.py:24
  535.7 5.6 collective-permute-start.17
  541.3 7.5 collective-permute-done.17
  550.3 3.1 collective-permute-start.18
  553.4 4.3 collective-permute-done.18
  560.0 2.7 collective-permute-done.19
  562.7 4.3 collective-permute-start.20
  567.9 7.3 collective-permute-start.21
  576.2 5.6 collective-permute-start.22
  581.8 7.5 collective-permute-done.22
  589.2 3.1 collective-permute-start.23
  593.8 4.6 collective-permute-start.24
  598.5 2.7 collective-permute-done.24
  603.3 2.4 collective-permute-done.25
  605.7 4.2 collective-permute-start.26
  611.0 7.3 collective-permute-start.27
  619.2 5.6 collective-permute-start.28
  624.8 7.4 collective-permute-done.28
  632.2 3.1 collective-permute-start.29
  636.6 4.6 collective-permute-start.30
  642.8 10.5 %all_gather.14 = bf16[4,32,768]{2,1,0:T(8,128)(2,1)} all-gather(bf16[1,32,768]{2,1,0:T(8,128)(2,1)S(1)} %fusion.39), channel_id=1, replica_groups=mesh['dp_0'=4,'dp_1'=16,'expert_0'=4,'expert_1'=2] {'dp_0'}, dimensions={0}, use_global_device_ids=true | all-gather | bytes 245760 | tf_op jit(solution)/shard_map/all_gather | solution.py:36
  653.3 87.5 %all-gather.5.cloned.1.call-done = bf16[64,32,768]{2,1,0:T(8,128)(2,1)} async-done(((bf16[4,32,768]{2,1,0:T(8,128)(2,1)}), bf16[64,32,768]{2,1,0:T(8,128)(2,1)}) %all-gather.5.cloned.1.call-update) | async-done | bytes 3145744 | tf_op jit(solution)/shard_map/all_gather | solution.py:36
  740.8 2.2 copy.64
  744.1 13.4 %all_to_all.35 = bf16[4,2,16,2048]{3,2,0,1:T(8,128)(2,1)S(1)} all-to-all(bf16[4,2,16,2048]{3,2,0,1:T(8,128)(2,1)S(1)} %copy.65), channel_id=1, replica_groups=mesh['dp_0'=4,'dp_1'=16,'expert_0'=4,'expert_1'=2] {'expert_1'}, dimensions={1} | all-to-all | bytes 1048576 | tf_op jit(solution)/shard_map/all_to_all | solution.py:57
  758.3 4.2 all-to-all-start.3
  763.7 6.0 all-to-all-done.3
  (144 shorter events, 57.0 us)
Async XLA Ops:
  7.2 15.0 %copy-start = (bf16[64,2048]{1,0:T(8,128)(2,1)S(1)}, bf16[64,2048]{1,0:T(8,128)(2,1)}, u32[]{:S(2)}) copy-start(bf16[64,2048]{1,0:T(8,128)(2,1)} %param.12) | copy-start | bytes 786436
  7.2 144.9 %all-gather.3.cloned.1.call-start = ((), (), s32[]{:S(2)}) async-start(), calls=%async_computation.4 | async-start | bytes 10027008 | tf_op jit(solution)/shard_map/all_gather | solution.py:36
  22.2 1.0 copy-start.2
  23.2 1.0 copy-start.15
  43.0 26.0 %all-to-all-start = ((bf16[8,16,2048]{2,1,0:T(8,128)(2,1)}), bf16[8,16,2048]{2,1,0:T(8,128)(2,1)S(1)}, u32[]{:S(2)}, u32[]{:S(2)}) async-start(bf16[8,16,2048]{2,1,0:T(8,128)(2,1)} %bitcast.1), calls=%async_computation | async-start | bytes 1048576 | tf_op jit(solution)/shard_map/all_to_all | solution.py:130
  49.1 691.6 %all-gather.5.cloned.1.call-start = ((), (), s32[]{:S(2)}) async-start(), calls=%async_computation.5 | async-start | bytes 3342336 | tf_op jit(solution)/shard_map/all_gather | solution.py:36
  58.2 5.4 copy-start.7
  66.9 112.5 %collective-permute-start.3 = (bf16[128,1024]{0,1:T(8,128)(2,1)}, bf16[128,1024]{0,1:T(8,128)(2,1)}, u32[]{:S(2)}, u32[]{:S(2)}) collective-permute-start(bf16[128,1024]{0,1:T(8,128)(2,1)} %bitcast.24), channel_id=1, source_target_pairs={{0,8},{8,0},{16,24},{24,16},{32,40},{40,32},{48,56},{56,48},{64,72... | collective-permute-start | bytes 786440 | tf_op jit(solution)/shard_map/ppermute | solution.py:24
  78.1 4.8 copy-start.6
  86.2 90.5 %collective-permute-start = (bf16[128,1024]{0,1:T(8,128)(2,1)}, bf16[128,1024]{0,1:T(8,128)(2,1)S(1)}, u32[]{:S(2)}, u32[]{:S(2)}) collective-permute-start(bf16[128,1024]{0,1:T(8,128)(2,1)} %bitcast.200), channel_id=1, source_target_pairs={{0,8},{8,0},{16,24},{24,16},{32,40},{40,32},{48,56},{56,48},{64,72... | collective-permute-start | bytes 786440 | tf_op jit(solution)/shard_map/ppermute | solution.py:24
  166.7 9.4 %copy-start.11 = (bf16[128,32,1,32]{0,3,1,2:T(8,128)(2,1)S(1)}, bf16[128,32,1,32]{0,3,1,2:T(8,128)(2,1)}, u32[]{:S(2)}) copy-start(bf16[128,32,1,32]{0,3,1,2:T(8,128)(2,1)} %copy.55) | copy-start | bytes 786436
  166.8 12.1 %collective-permute-start.1 = (bf16[128,768]{1,0:T(8,128)(2,1)S(1)}, bf16[128,768]{1,0:T(8,128)(2,1)S(1)}, u32[]{:S(2)}, u32[]{:S(2)}) collective-permute-start(bf16[128,768]{1,0:T(8,128)(2,1)S(1)} %get-tuple-element.53), channel_id=1, source_target_pairs={{0,8},{8,0},{16,24},{24,16},{32,40},{40,32},{48,56},{56,48},{64,72... | collective-permute-start | bytes 589832 | tf_op jit(solution)/shard_map/ppermute | solution.py:24
  169.5 8.8 %collective-permute-start.2 = (bf16[128,768]{1,0:T(8,128)(2,1)S(1)}, bf16[128,768]{1,0:T(8,128)(2,1)S(1)}, u32[]{:S(2)}, u32[]{:S(2)}) collective-permute-start(bf16[128,768]{1,0:T(8,128)(2,1)S(1)} %get-tuple-element.55), channel_id=1, source_target_pairs={{0,8},{8,0},{16,24},{24,16},{32,40},{40,32},{48,56},{56,48},{64,72... | collective-permute-start | bytes 589832 | tf_op jit(solution)/shard_map/ppermute | solution.py:24
  173.3 9.2 %collective-permute-start.4 = (bf16[128,768]{1,0:T(8,128)(2,1)S(1)}, bf16[128,768]{1,0:T(8,128)(2,1)S(1)}, u32[]{:S(2)}, u32[]{:S(2)}) collective-permute-start(bf16[128,768]{1,0:T(8,128)(2,1)S(1)} %get-tuple-element.54), channel_id=1, source_target_pairs={{0,8},{8,0},{16,24},{24,16},{32,40},{40,32},{48,56},{56,48},{64,72... | collective-permute-start | bytes 589832 | tf_op jit(solution)/shard_map/ppermute | solution.py:24
  187.8 4.3 collective-permute-start.5
  194.3 2.9 copy-start.3
  197.2 106.7 %collective-permute-start.6 = (bf16[3,16,32,768]{3,2,1,0:T(8,128)(2,1)}, bf16[3,16,32,768]{3,2,1,0:T(8,128)(2,1)S(1)}, u32[]{:S(2)}, u32[]{:S(2)}) collective-permute-start(bf16[3,16,32,768]{3,2,1,0:T(8,128)(2,1)} %dynamic-slice_bitcast_fusion), channel_id=1, source_target_pairs={{0,16},{8,24},{16,0},{24,8},{32,48},{40,56},{48,32},{56,40},{64,80... | collective-permute-start | bytes 7077896 | tf_op jit(solution)/shard_map/ppermute | solution.py:24
  201.7 116.0 %copy-start.4 = (bf16[3,16,2,32,768]{4,3,1,0,2:T(8,128)(2,1)S(1)}, bf16[3,16,2,32,768]{4,3,1,0,2:T(8,128)(2,1)}, u32[]{:S(2)}) copy-start(bf16[3,16,2,32,768]{4,3,1,0,2:T(8,128)(2,1)} %copy-done.3) | copy-start | bytes 14155780
  303.9 4.2 copy-start.5
  308.1 4.3 collective-permute-start.7
  312.5 5.2 collective-permute-start.8
  321.6 109.8 %collective-permute-start.9 = (bf16[3,8,32,768]{3,2,1,0:T(8,128)(2,1)}, bf16[3,8,32,768]{3,2,1,0:T(8,128)(2,1)}, u32[]{:S(2)}, u32[]{:S(2)}) collective-permute-start(bf16[3,8,32,768]{3,2,1,0:T(8,128)(2,1)} %dynamic-slice_bitcast_fusion.1), channel_id=1, source_target_pairs={{0,32},{8,40},{16,48},{24,56},{32,0},{40,8},{48,16},{56,24},{64,96... | collective-permute-start | bytes 3538952 | tf_op jit(solution)/shard_map/ppermute | solution.py:24
  433.6 4.3 collective-permute-start.10
  437.9 5.2 collective-permute-start.11
  443.1 8.2 %collective-permute-start.12 = (f32[3,3]{1,0:T(4,128)S(1)}, f32[3,3]{1,0:T(4,128)S(1)}, u32[]{:S(2)}, u32[]{:S(2)}) collective-permute-start(f32[3,3]{1,0:T(4,128)S(1)} %fusion.128), channel_id=1, source_target_pairs={{0,32},{8,40},{16,48},{24,56},{32,0},{40,8},{48,16},{56,24},{64,96... | collective-permute-start | bytes 116 | tf_op jit(solution)/shard_map/ppermute | solution.py:24
  453.2 1.0 copy-start.8
  454.2 99.2 %copy-start.14 = (f32[1,32,768]{2,1,0:T(8,128)S(1)}, f32[1,32,768]{2,1,0:T(8,128)}, u32[]{:S(2)}) copy-start(f32[1,32,768]{2,1,0:T(8,128)} %param.15) | copy-start | bytes 294916
  454.3 44.5 %collective-permute-start.13 = (bf16[3,4,32,768]{3,2,1,0:T(8,128)(2,1)S(1)}, bf16[3,4,32,768]{3,2,1,0:T(8,128)(2,1)S(1)}, u32[]{:S(2)}, u32[]{:S(2)}) collective-permute-start(bf16[3,4,32,768]{3,2,1,0:T(8,128)(2,1)S(1)} %dynamic-slice_bitcast_fusion.2), channel_id=1, source_target_pairs={{0,64},{8,72},{16,80},{24,88},{32,96},{40,104},{48,112},{56,120},{... | collective-permute-start | bytes 1769480 | tf_op jit(solution)/shard_map/ppermute | solution.py:24
  500.3 98.1 %copy-start.13 = (f32[1,32,768]{2,1,0:T(8,128)S(1)}, f32[1,32,768]{2,1,0:T(8,128)}, u32[]{:S(2)}) copy-start(f32[1,32,768]{2,1,0:T(8,128)} %param.16) | copy-start | bytes 294916
  500.3 98.1 %copy-start.12 = (f32[1,32,768]{2,1,0:T(8,128)S(1)}, f32[1,32,768]{2,1,0:T(8,128)}, u32[]{:S(2)}) copy-start(f32[1,32,768]{2,1,0:T(8,128)} %param.17) | copy-start | bytes 294916
  500.3 14.0 %collective-permute-start.14 = (f32[3,3]{1,0:T(4,128)S(1)}, f32[3,3]{1,0:T(4,128)S(1)}, u32[]{:S(2)}, u32[]{:S(2)}) collective-permute-start(f32[3,3]{1,0:T(4,128)S(1)} %pad_maximum_fusion.8), channel_id=1, source_target_pairs={{0,8},{8,0},{16,24},{24,16},{32,40},{40,32},{48,56},{56,48},{64,72... | collective-permute-start | bytes 116 | tf_op jit(solution)/shard_map/ppermute | solution.py:24
  514.3 5.2 collective-permute-start.15
  519.6 16.2 %collective-permute-start.16 = (f32[3,3]{1,0:T(4,128)S(1)}, f32[3,3]{1,0:T(4,128)S(1)}, u32[]{:S(2)}, u32[]{:S(2)}) collective-permute-start(f32[3,3]{1,0:T(4,128)S(1)} %fusion.127), channel_id=1, source_target_pairs={{0,32},{8,40},{16,48},{24,56},{32,0},{40,8},{48,16},{56,24},{64,96... | collective-permute-start | bytes 116 | tf_op jit(solution)/shard_map/ppermute | solution.py:24
  535.7 13.0 %collective-permute-start.17 = (f32[3,3]{1,0:T(4,128)S(1)}, f32[3,3]{1,0:T(4,128)S(1)}, u32[]{:S(2)}, u32[]{:S(2)}) collective-permute-start(f32[3,3]{1,0:T(4,128)S(1)} %add.353), channel_id=1, source_target_pairs={{0,64},{8,72},{16,80},{24,88},{32,96},{40,104},{48,112},{56,120},{... | collective-permute-start | bytes 116 | tf_op jit(solution)/shard_map/ppermute | solution.py:24
  548.8 93.6 %copy-start.9 = (f32[1,3,32,768]{3,2,1,0:T(8,128)S(1)}, f32[1,3,32,768]{3,2,1,0:T(8,128)}, u32[]{:S(2)}) copy-start(f32[1,3,32,768]{3,2,1,0:T(8,128)} %param.18) | copy-start | bytes 884740
  548.8 93.6 %copy-start.10 = (f32[1,3,32,768]{3,2,1,0:T(8,128)S(1)}, f32[1,3,32,768]{3,2,1,0:T(8,128)}, u32[]{:S(2)}) copy-start(f32[1,3,32,768]{3,2,1,0:T(8,128)} %param.19) | copy-start | bytes 884740
  550.3 7.5 collective-permute-start.18
  558.0 4.6 collective-permute-start.19
  562.7 5.2 collective-permute-start.20
  567.9 8.3 %collective-permute-start.21 = (f32[3,3]{1,0:T(4,128)S(1)}, f32[3,3]{1,0:T(4,128)S(1)}, u32[]{:S(2)}, u32[]{:S(2)}) collective-permute-start(f32[3,3]{1,0:T(4,128)S(1)} %fusion.126), channel_id=1, source_target_pairs={{0,32},{8,40},{16,48},{24,56},{32,0},{40,8},{48,16},{56,24},{64,96... | collective-permute-start | bytes 116 | tf_op jit(solution)/shard_map/ppermute | solution.py:24
  576.2 13.0 %collective-permute-start.22 = (f32[3,3]{1,0:T(4,128)S(1)}, f32[3,3]{1,0:T(4,128)S(1)}, u32[]{:S(2)}, u32[]{:S(2)}) collective-permute-start(f32[3,3]{1,0:T(4,128)S(1)} %add.362), channel_id=1, source_target_pairs={{0,64},{8,72},{16,80},{24,88},{32,96},{40,104},{48,112},{56,120},{... | collective-permute-start | bytes 116 | tf_op jit(solution)/shard_map/ppermute | solution.py:24
  589.2 4.3 collective-permute-start.23
  593.8 7.4 collective-permute-start.24
  601.4 4.3 collective-permute-start.25
  605.7 5.2 collective-permute-start.26
  611.0 8.2 %collective-permute-start.27 = (f32[3,3]{1,0:T(4,128)S(1)}, f32[3,3]{1,0:T(4,128)S(1)}, u32[]{:S(2)}, u32[]{:S(2)}) collective-permute-start(f32[3,3]{1,0:T(4,128)S(1)} %fusion.125), channel_id=1, source_target_pairs={{0,32},{8,40},{16,48},{24,56},{32,0},{40,8},{48,16},{56,24},{64,96... | collective-permute-start | bytes 116 | tf_op jit(solution)/shard_map/ppermute | solution.py:24
  619.2 13.0 %collective-permute-start.28 = (f32[3,3]{1,0:T(4,128)S(1)}, f32[3,3]{1,0:T(4,128)S(1)}, u32[]{:S(2)}, u32[]{:S(2)}) collective-permute-start(f32[3,3]{1,0:T(4,128)S(1)} %add.372), channel_id=1, source_target_pairs={{0,64},{8,72},{16,80},{24,88},{32,96},{40,104},{48,112},{56,120},{... | collective-permute-start | bytes 116 | tf_op jit(solution)/shard_map/ppermute | solution.py:24
  632.2 4.3 collective-permute-start.29
  636.6 5.8 collective-permute-start.30
  757.5 13.1 %copy-start.1 = (bf16[64,2048]{1,0:T(8,128)(2,1)S(1)}, bf16[64,2048]{1,0:T(8,128)(2,1)}, u32[]{:S(2)}) copy-start(bf16[64,2048]{1,0:T(8,128)(2,1)} %param.12) | copy-start | bytes 786436
  758.3 11.4 %all-to-all-start.3 = ((bf16[4,2,16,2048]{3,2,1,0:T(8,128)(2,1)}), bf16[4,2,16,2048]{3,2,1,0:T(8,128)(2,1)S(1)}, u32[]{:S(2)}, u32[]{:S(2)}) async-start(bf16[4,2,16,2048]{3,2,1,0:T(8,128)(2,1)} %copy.66), calls=%async_computation.3 | async-start | bytes 1048576 | tf_op jit(solution)/shard_map/all_to_all | solution.py:57
Sparse Core Ops, SparseCore 0:
  20.8 131.1 all-gather.2
  653.4 87.3 all-gather.4
where the time goes:
time: 782 us; the launch traced here: 777 us
  waiting for transfers between devices  460 us (59%)
  starting transfers between devices  157 us (20%)
  local copies, waits for them, and re-layouts  58.5 us (7%)
  blocking collectives  54.1 us (7%)
  other arithmetic  24.9 us (3%)
  between operations  14.8 us (2%)
  matrix products  8.3 us (1%)
    ppermute x31, waiting for transfers between devices, swapped(): lax.ppermute(array, axis, [(i, i ^ 1 << apart) for i in range(lax.axis_si...  304 us
    all_gather x2, waiting for transfers between devices, all_blocks(): parts = lax.all_gather(parts, axes[k], axis=0, tiled=True)  150 us
    ppermute x31, starting transfers between devices, swapped(): lax.ppermute(array, axis, [(i, i ^ 1 << apart) for i in range(lax.axis_si...  147 us
    dynamic_slice x6, local copies, waits for them, and re-layouts, half_columns(): chosen = lax.dynamic_index_in_dim(shaped, selected, 2, keepdims=False)  31.7 us
    all_gather x2, blocking collectives, all_blocks(): parts = lax.all_gather(parts, axes[k], axis=0, tiled=True)  22.9 us
    all_to_all x1, blocking collectives, shards(): lax.all_to_all(sent_grads, EXPERT, split_axis=0, concat_axis=0, tiled=True)  17.8 us
  transfers between devices with their start and end apart: 35, of which 31 were waited for; matrix products, arithmetic and copies ran while one was open for 7% of the time, Pallas kernels for 0%

commit v1 on v0

v1 whole, which is shorter than its diff:
```python
import functools

import jax
import jax.numpy as jnp
from jax import lax
from jax.experimental import pallas as pl
from jax.experimental.pallas import tpu as pltpu
from jax.sharding import Mesh
from jax.sharding import PartitionSpec as P

AXES = ("y", "t", "l", "x", "c")
DP = ("y", "t", "l")
EXPERT = ("x", "c")
MESH_ID = pl.DeviceIdType.MESH

first_decay = 0.9
second_decay = 0.95
learn_rate = 0.01
adam_eps = 1e-08
weight_decay = 0.1
adam_count = 100.0
norm_eps = 1e-06
ANY = pl.BlockSpec(memory_space=pl.ANY)
VMEM = pl.BlockSpec(memory_space=pltpu.VMEM)
DMA = pltpu.SemaphoreType.DMA


def place():
    return tuple(lax.axis_index(a) for a in AXES)


def remote(src, dst, send_sem, recv_sem, dev):
    return pltpu.make_async_remote_copy(
        src_ref=src,
        dst_ref=dst,
        send_sem=send_sem,
        recv_sem=recv_sem,
        device_id=dev,
        device_id_type=MESH_ID,
    )


def full(dev):
    return {a: dev[a] if a in dev else lax.axis_index(a) for a in AXES}


def is_self(dev):
    same = None
    for a in AXES:
        if a in dev:
            eq = lax.axis_index(a) == dev[a]
            same = eq if same is None else jnp.logical_and(same, eq)
    return same


def greet(others, maybe_self):
    barrier = pltpu.get_barrier_semaphore()
    for dev in others:
        pl.semaphore_signal(barrier, inc=1, device_id=dev, device_id_type=MESH_ID)
    for dev in maybe_self:
        pl.semaphore_signal(barrier, inc=1, device_id=dev, device_id_type=MESH_ID)
    pl.semaphore_wait(barrier, len(others) + len(maybe_self))


def send_or_copy(src, dst, send_sem, recv_sem, dev):
    mine = is_self(dev)

    @pl.when(mine)
    def _():
        pltpu.make_async_copy(src, dst, recv_sem).start()

    @pl.when(jnp.logical_not(mine))
    def _():
        remote(src, dst, send_sem, recv_sem, dev).start()


def wait_sent(src, dst, send_sem, recv_sem, dev):
    @pl.when(jnp.logical_not(is_self(dev)))
    def _():
        remote(src, dst, send_sem, recv_sem, dev).wait_send()


def landed(ref, recv_sem):
    pltpu.make_async_copy(ref, ref, recv_sem).wait()


def worker_of_rows(e):
    y, t, l, x, c = place()
    return {"t": e, "l": t % 2, "x": (t // 2 + e) % 4, "c": l}


def tree_place(x, t):
    return (x + 8 - t) % 4


def source_of_rows(s):
    y, t, l, x, c = place()
    return {"t": 2 * tree_place(x, t) + l, "l": c, "x": s // 2, "c": s % 2}


def row_x(x, t):
    return (x + 8 - t // 2 - 2 * (t % 2)) % 4


def relay_shift():
    t, c = lax.axis_index("t"), lax.axis_index("c")
    return (t + 2 * c) % 4


def relay_to():
    return {"x": (lax.axis_index("x") + relay_shift()) % 4}


def relay_from():
    return {"x": (lax.axis_index("x") + 4 - relay_shift()) % 4}


def block_expert():
    return 2 * relay_from()["x"] + lax.axis_index("c")


def worker_of_block(h):
    return {"t": block_expert(), "l": lax.axis_index("t") // 4, "c": h}


def sender_of_block(k):
    y, t, l, x, c = place()
    return {"t": 4 * l + row_x(x, t), "l": k, "c": t % 2}


def block_of_owner(h):
    y, t, l, x, c = place()
    return {"t": 2 * x + c, "l": t // 4, "x": relay_to()["x"], "c": h}


def owner_of_block(k):
    y, t, l, x, c = place()
    return {"t": 4 * l + row_x(x, t), "l": k, "x": t // 2, "c": t % 2}


def ring(axis, step):
    return {axis: (lax.axis_index(axis) + step) % 4}


def gather_peers():
    l = lax.axis_index("l")
    return [{"l": 1 - l}, ring("x", 1), ring("x", 3), ring("y", 1), ring("y", 3)]


def gather_swap(g, send, recv):
    y, t, l, x, c = place()
    mine = g.at[:, y, l, row_x(x, t)]
    swap = remote(mine, mine, send.at[0], recv.at[0], {"l": 1 - l})
    swap.start()
    return swap


def gather_block(g, swap, send, recv):
    y, t, l, x, c = place()
    rows = g.shape[4] // 2
    first, last = pl.ds(0, rows), pl.ds(rows, rows)
    swap.wait_send()
    landed(g.at[:, y, 1 - l, row_x(x, t)], recv.at[0])

    def start_ring(axis, parts, base):
        at = lax.axis_index(axis)
        for k, step in ((0, 1), (1, 3)):
            part = parts(at, 0, 2)
            remote(part, part, send.at[base + k], recv.at[base + k], ring(axis, step)).start()

    def relay_ring(axis, parts, base):
        at = lax.axis_index(axis)
        for k, step in ((0, 1), (1, 3)):
            came = (at + 4 - step) % 4
            landed(parts(came, 0, 2), recv.at[base + k])
            part = parts(came, k, 1)
            remote(part, part, send.at[base + 2 + k], recv.at[base + 2 + k], ring(axis, step)).start()

    def end_ring(axis, parts, base):
        at = lax.axis_index(axis)
        for k, step in ((0, 1), (1, 3)):
            part = parts(at, 0, 2)
            remote(part, part, send.at[base + k], recv.at[base + k], ring(axis, step)).wait_send()
            part = parts((at + 4 - step) % 4, k, 1)
            remote(part, part, send.at[base + 2 + k], recv.at[base + 2 + k], ring(axis, step)).wait_send()
            landed(parts((at + 2) % 4, k, 1), recv.at[base + 2 + k])

    def x_one(at, k, n):
        return g.at[:, y, pl.ds(k, n), row_x(at, t), first]

    def y_one(at, k, n):
        return g.at[:, at, pl.ds(k, n), row_x(x, t), last]

    def y_all(at, k, n):
        return g.at[:, at, pl.ds(k, n), :, first]

    def x_all(at, k, n):
        return g.at[:, :, pl.ds(k, n), row_x(at, t), last]

    for one, two, base in ((("x", x_one), ("y", y_one), 1), (("y", y_all), ("x", x_all), 9)):
        start_ring(*one, base)
        start_ring(*two, base + 4)
        relay_ring(*one, base)
        relay_ring(*two, base + 4)
        end_ring(*one, base)
        end_ring(*two, base + 4)


GATHER_SEMS = 17


def dispatch_kernel(tok, grd, wts, xt, xg, g, relay, s_row, r_row, s_fwd, r_fwd, s_rl, r_rl, s_wt, r_wt, s_g, r_g):
    y, t, l, x, c = place()
    other = {"c": 1 - c}
    greet(
        [other] + gather_peers(),
        [worker_of_rows(e) for e in range(8)]
        + [source_of_rows(s) for s in range(8)]
        + [worker_of_block(h) for h in range(2)]
        + [sender_of_block(k) for k in range(2)]
        + [relay_to(), relay_from()],
    )
    to_relay = (wts, relay, s_rl, r_rl, relay_to())
    send_or_copy(*to_relay)
    landed(relay, r_rl)
    chunk = g.at[:, y, t // 4, t % 4, pl.ds(pl.multiple_of(l * 32, 32), 32)]
    weight_sends = [(relay.at[h], chunk, s_wt.at[h], r_wt.at[l], worker_of_block(h)) for h in range(2)]
    for a in weight_sends:
        send_or_copy(*a)
    mine = g.at[:, y, l, row_x(x, t)]
    for k in range(2):
        landed(mine.at[:, pl.ds(32 * k, 32)], r_wt.at[k])
    swap = gather_swap(g, s_g, r_g)
    row_sends = []
    slot = 2 * x + c
    for src, dst, which in ((tok, xt, 0), (grd, xg, 1)):
        for e in range(8):
            row_sends.append(
                (src.at[e], dst.at[l, slot], s_row.at[which, e], r_row.at[which, slot], worker_of_rows(e))
            )
    for a in row_sends:
        send_or_copy(*a)
    gather_block(g, swap, s_g, r_g)
    forwards = []
    for dst, which in ((xt, 0), (xg, 1)):
        for s in range(8):
            landed(dst.at[c, s], r_row.at[which, s])
            f = remote(dst.at[c, s], dst.at[c, s], s_fwd.at[which, s], r_fwd.at[which, s], other)
            f.start()
            forwards.append(f)
    for a in [to_relay] + weight_sends + row_sends:
        wait_sent(*a)
    for f in forwards:
        f.wait_send()
    for dst, which in ((xt, 0), (xg, 1)):
        for s in range(8):
            landed(dst.at[1 - c, s], r_fwd.at[which, s])


PAIRS = [(i, k) for i in range(4) for k in range(i, 4)]
LAST = (((1,), (1,)), ((), ()))


def pair_kernel(xt, xg, hid, state, ft, fg, fh, relay, tile, lines, box, send, recv, own, sb, rb, s_rl, r_rl):
    y, t, l, x, c = place()
    across, other = {"l": 1 - l}, {"c": 1 - c}
    peers = small_peers(False)
    greet([across, other] + peers, [relay_to(), relay_from()])
    mine = 2 * l
    theirs = 2 * (1 - l)
    first, local, second = [], [], []
    for k, (src, dst) in enumerate(((xt, ft), (xg, fg))):
        for n in range(4):
            cols = pl.ds(256 * n, 256)
            theirs_half = pl.ds(pl.multiple_of(512 * n + (1 - l) * 256, 256), 256)
            my_half = pl.ds(pl.multiple_of(512 * n + l * 256, 256), 256)
            first.append(
                remote(src.at[c, :, theirs_half], dst.at[mine + c, :, cols], send.at[k, n], recv.at[k, n], across)
            )
            local.append(pltpu.make_async_copy(src.at[:, :, my_half], dst.at[pl.ds(mine, 2), :, cols], own.at[k, n]))
    first.append(remote(hid, fh.at[:, pl.ds(mine, 2)], send.at[2, 0], recv.at[2, 0], across))
    local.append(pltpu.make_async_copy(hid, fh.at[:, pl.ds(mine, 2)], own.at[2, 0]))
    for f in first:
        f.start()
    to_relay = (state, relay, s_rl, r_rl, relay_to())
    send_or_copy(*to_relay)
    for f in local:
        f.start()
    for k, dst in ((0, ft), (1, fg)):
        for n in range(4):
            piece = dst.at[theirs + c, :, pl.ds(256 * n, 256)]
            landed(piece, recv.at[k, n])
            f = remote(piece, piece, send.at[3 + k, n], recv.at[3 + k, n], other)
            f.start()
            second.append(f)
    for f in local:
        f.wait()
    landed(fh.at[:, pl.ds(theirs, 2)], recv.at[2, 0])
    for f in first:
        f.wait_send()
    wait_sent(*to_relay)
    landed(relay, r_rl)
    for f in second:
        f.wait_send()
    for k, dst in ((0, ft), (1, fg)):
        for n in range(4):
            landed(dst.at[theirs + 1 - c, :, pl.ds(256 * n, 256)], recv.at[3 + k, n])
    lines[...] = jnp.zeros_like(lines)
    for n, (i, k) in enumerate(PAIRS):
        both_t = lax.dot_general(ft[i], ft[k], LAST, preferred_element_type=jnp.float32)
        both_g = lax.dot_general(fg[i], fg[k], LAST, preferred_element_type=jnp.float32)
        for m, both in ((0, both_t), (1, both_t), (2, both_g)):
            inner = lax.dot_general(fh[m, i], fh[m, k], LAST, preferred_element_type=jnp.float32)
            lines[pl.ds(10 * m + n, 1), :] = jnp.sum(both * inner, axis=0, keepdims=True)
    total = jnp.broadcast_to(jnp.sum(lines[...], axis=1, keepdims=True), (32, 128))
    tile[...] = small_sum(total, box, peers, 2 * l + c, sb, rb)


def small_peers(with_x):
    y, t, l, x, c = place()
    out = []
    for dx in range(4 if with_x else 1):
        for dl in range(2):
            for dc in range(2):
                if dx + dl + dc > 0:
                    out.append({"x": (x + dx) % 4, "l": (l + dl) % 2, "c": (c + dc) % 2})
    return out


def small_sum(part, box, peers, at, send, recv):
    box[at] = part
    sends = []
    for k, dev in enumerate(peers):
        f = remote(box.at[at], box.at[at], send.at[k], recv.at[k], dev)
        f.start()
        sends.append(f)
    for k in range(len(peers)):
        landed(box.at[at], recv.at[k])
    for f in sends:
        f.wait_send()
    return jnp.sum(box[...], axis=0)


def gram_tile(r, lines):
    rows = r.shape[2]
    lines[...] = jnp.zeros_like(lines)
    for m in range(3):

        def step(i, accs, m=m):
            at = pl.ds(pl.multiple_of(i * 16, 16), 16)
            parts = [r[k, m, at, :].astype(jnp.float32) for k in range(4)]
            out = []
            for n, (i1, i2) in enumerate(PAIRS):
                prod = parts[i1] * parts[i2]
                out.append(accs[n] + (prod[:8] + prod[8:]))
            return tuple(out)

        zero = tuple(jnp.zeros((8, 384), jnp.float32) for _ in PAIRS)
        accs = lax.fori_loop(0, rows // 16, step, zero)
        for n, acc in enumerate(accs):
            line = jnp.sum(acc, axis=0, keepdims=True)
            lines[pl.ds(10 * m + n, 1), :] = line[:, :128] + line[:, 128:256] + line[:, 256:]
    return jnp.broadcast_to(jnp.sum(lines[...], axis=1, keepdims=True), (32, 128))


def ring_kernel(axis, *refs):
    if axis == "x":
        v, state, r, gram, got_state, relay, lines, box, sv, rv, own, sb, rb, ss, rs = refs
    else:
        v, r, gram, relay, lines, box, box2, sv, rv, own, sb, rb, sb2, rb2 = refs
    y, t, l, x, c = place()
    at = lax.axis_index(axis)
    rows = r.shape[2]
    peers = small_peers(True)
    up, down = ring(axis, 1), ring(axis, 3)
    others = [up, down] + peers
    maybe = []
    if axis == "x":
        maybe = [worker_of_block(h) for h in range(2)] + [sender_of_block(k) for k in range(2)]
    else:
        others = others + [ring("y", k) for k in range(1, 4)]
    greet(others, maybe)
    low, high = pl.ds(0, rows // 2), pl.ds(rows // 2, rows // 2)
    far, nxt, prv = (at + 2) % 4, (at + 1) % 4, (at + 3) % 4

    def part(p):
        return v.at[row_x(p, t) if axis == "x" else p]

    def slot(p):
        return r.at[tree_place(p, t) if axis == "x" else p]

    first = [
        remote(part(far).at[:, low], relay.at[0], sv.at[0], rv.at[0], up),
        remote(part(far).at[:, high], relay.at[1], sv.at[1], rv.at[1], down),
        remote(part(nxt), slot(at), sv.at[2], rv.at[2], up),
        remote(part(prv), slot(at), sv.at[3], rv.at[3], down),
    ]
    for f in first:
        f.start()
    keep = pltpu.make_async_copy(part(at), slot(at), own)
    keep.start()
    sends = []
    if axis == "x":
        piece = pl.ds(pl.multiple_of(l * 32, 32), 32)
        for h in range(2):
            sends.append((state.at[h], got_state.at[:, piece], ss.at[h], rs.at[l], worker_of_block(h)))
        for a in sends:
            send_or_copy(*a)
    landed(relay.at[0], rv.at[0])
    fwd_up = remote(relay.at[0], slot(prv).at[:, low], sv.at[4], rv.at[4], up)
    fwd_up.start()
    landed(relay.at[1], rv.at[1])
    fwd_down = remote(relay.at[1], slot(nxt).at[:, high], sv.at[5], rv.at[5], down)
    fwd_down.start()
    keep.wait()
    landed(slot(prv), rv.at[2])
    landed(slot(nxt), rv.at[3])
    landed(slot(far).at[:, low], rv.at[4])
    landed(slot(far).at[:, high], rv.at[5])
    for f in first + [fwd_up, fwd_down]:
        f.wait_send()
    total = small_sum(gram_tile(r, lines), box, peers, x * 4 + l * 2 + c, sb, rb)
    if axis == "y":
        total = small_sum(total, box2, [ring("y", k) for k in range(1, 4)], y, sb2, rb2)
    gram[...] = total
    if axis == "x":
        for a in sends:
            wait_sent(*a)
        for k in range(2):
            landed(got_state.at[:, pl.ds(32 * k, 32)], rs.at[k])


def final_kernel(mine, comb, hid, ret, got, g, part, came, rounded, own, s_g, r_g, s_c, r_c, s_p, r_p, s_y, r_y):
    y, t, l, x, c = place()
    other = {"c": 1 - c}
    greet(
        [other] + gather_peers(),
        [block_of_owner(h) for h in range(2)]
        + [owner_of_block(k) for k in range(2)]
        + [worker_of_rows(e) for e in range(8)]
        + [source_of_rows(s) for s in range(8)],
    )
    keep = pltpu.make_async_copy(mine, g.at[:, y, l, row_x(x, t)], own)
    keep.start()
    col = pl.ds(pl.multiple_of(c * 384, 384), 384)
    sends = []
    for k in range(2):
        sends.append(
            (
                comb.at[:, pl.ds(32 * k, 32)],
                got.at[:, :, col],
                s_c.at[k],
                r_c.at[c],
                owner_of_block(k),
            )
        )
    keep.wait()
    swap = gather_swap(g, s_g, r_g)
    for a in sends:
        send_or_copy(*a)
    gather_block(g, swap, s_g, r_g)
    for n in range(8):
        rows = g[0, n // 2, n % 2].reshape(256, 384)
        for k in range(2):
            block = lax.dot_general(hid[k], rows, LAST, preferred_element_type=jnp.float32)
            part[k, :, :, pl.ds(256 * n, 256)] = block.reshape(8, 16, 256)
    swaps = []
    for s in range(8):
        f = remote(part.at[1 - c, s], came.at[s], s_p.at[s], r_p.at[s], other)
        f.start()
        swaps.append(f)
    backs = []
    for s in range(8):
        landed(came.at[s], r_p.at[s])
        rounded[s] = (part[c, s] + came[s]).astype(jnp.bfloat16)
        a = (rounded.at[s], ret.at[t], s_y.at[s], r_y.at[t], source_of_rows(s))
        send_or_copy(*a)
        backs.append(a)
    for f in swaps:
        f.wait_send()
    for a in sends + backs:
        wait_sent(*a)
    for h in range(2):
        landed(got.at[:, :, pl.ds(384 * h, 384)], r_c.at[h])
    for e in range(8):
        landed(ret.at[e], r_y.at[e])


def call(kernel, outs, in_specs, out_specs, scratch, cid):
    return pl.pallas_call(
        kernel,
        out_shape=outs,
        in_specs=in_specs,
        out_specs=out_specs,
        scratch_shapes=scratch,
        compiler_params=pltpu.CompilerParams(
            collective_id=cid, has_side_effects=True, vmem_limit_bytes=48 * 1024 * 1024
        ),
    )


def shape(dims, kind=jnp.bfloat16):
    return jax.ShapeDtypeStruct(dims, kind)


def pair_coefs(cross, lower, upper):
    return (
        1.0 - cross / (2.0 * (lower + norm_eps)),
        1.0 - cross / (2.0 * (upper + norm_eps)),
    )


def quad_coefs(gram):
    a0, b0 = pair_coefs(gram[0][1], gram[0][0], gram[1][1])
    a1, b1 = pair_coefs(gram[2][3], gram[2][2], gram[3][3])
    lower = a0 * a0 * gram[0][0] + 2.0 * a0 * b0 * gram[0][1] + b0 * b0 * gram[1][1]
    upper = a1 * a1 * gram[2][2] + 2.0 * a1 * b1 * gram[2][3] + b1 * b1 * gram[3][3]
    cross = a0 * (a1 * gram[0][2] + b1 * gram[0][3]) + b0 * (a1 * gram[1][2] + b1 * gram[1][3])
    a2, b2 = pair_coefs(cross, lower, upper)
    return jnp.stack([a2 * a0, a2 * b0, b2 * a1, b2 * b1])


def tile_coefs(tile):
    sums = tile[:30, 0].reshape(3, 10)
    gram = [[None] * 4 for _ in range(4)]
    for n, (i, k) in enumerate(PAIRS):
        gram[i][k] = sums[:, n]
    return quad_coefs(gram)


def shards(
    tokens,
    cotangent,
    route,
    counts,
    gate_master,
    up_master,
    down_master,
    first_moment,
    second_moment,
):
    y, t, l, x, c = place()
    bf16, f32 = jnp.bfloat16, jnp.float32
    slot_ids = jnp.arange(128, dtype=jnp.int32)
    live_slots = slot_ids % 16 < jnp.repeat(counts[0], 16)
    sent_tokens = jnp.where(live_slots[:, None], jnp.take(tokens, route, axis=0), 0)
    sent_grads = jnp.where(live_slots[:, None], jnp.take(cotangent, route, axis=0), 0)
    masters = jnp.stack([gate_master[0], up_master[0], down_master[0]])
    halves = jnp.moveaxis(masters.astype(bf16).reshape(3, 32, 2, 384), 2, 0)
    xt, xg, weights, _ = call(
        dispatch_kernel,
        (
            shape((2, 8, 16, 2048)),
            shape((2, 8, 16, 2048)),
            shape((3, 4, 2, 4, 64, 384)),
            shape((2, 3, 32, 384)),
        ),
        [ANY] * 3,
        [ANY] * 4,
        [DMA((2, 8))] * 4 + [DMA(())] * 2 + [DMA((2,))] * 2 + [DMA((GATHER_SEMS,))] * 2,
        0,
    )(sent_tokens.reshape(8, 16, 2048), sent_grads.reshape(8, 16, 2048), halves)
    xt = xt.reshape(256, 2048)
    xg = xg.reshape(256, 2048)
    weights = weights.reshape(3, 2048, 384)
    gate_pre = jnp.dot(xt, weights[0], preferred_element_type=f32)
    up_pre = jnp.dot(xt, weights[1], preferred_element_type=f32)
    back_hidden = jnp.dot(xg, weights[2], preferred_element_type=f32)
    sigmoid_gate = jax.nn.sigmoid(gate_pre)
    active_gate = gate_pre * sigmoid_gate
    hidden = (active_gate * up_pre).astype(bf16)
    d_gate = (back_hidden * up_pre * sigmoid_gate * (1.0 + gate_pre * (1.0 - sigmoid_gate))).astype(bf16)
    d_up = (back_hidden * active_gate).astype(bf16)
    factors = jnp.stack([d_gate, d_up, hidden]).reshape(3, 2, 128, 384)
    state = jnp.stack([masters[2], first_moment[0, 2], second_moment[0, 2]])
    state = jnp.moveaxis(state.reshape(3, 32, 2, 384), 2, 0)
    four_t, four_g, four_h, state, tile = call(
        pair_kernel,
        (
            shape((4, 128, 1024)),
            shape((4, 128, 1024)),
            shape((3, 4, 128, 384)),
            shape((2, 3, 32, 384), f32),
            shape((32, 128), f32),
        ),
        [ANY] * 4,
        [VMEM] * 3 + [ANY, VMEM],
        [pltpu.VMEM((32, 128), f32), pltpu.VMEM((4, 32, 128), f32)]
        + [DMA((5, 4))] * 2
        + [DMA((3, 4))]
        + [DMA((3,))] * 2
        + [DMA(())] * 2,
        1,
    )(xt.reshape(2, 128, 2048), xg.reshape(2, 128, 2048), factors, state)
    coefs = tile_coefs(tile)
    four_t = four_t.reshape(512, 1024)
    four_g = four_g.reshape(512, 1024)
    scaled = four_h.astype(f32) * coefs.T[:, :, None, None]
    scaled = scaled.astype(bf16).reshape(3, 512, 384)
    rows_first = (((0,), (0,)), ((), ()))
    vec = jnp.stack(
        [
            lax.dot_general(src, scaled[m], rows_first, preferred_element_type=f32).astype(bf16)
            for m, src in ((0, four_t), (1, four_t), (2, four_g))
        ]
    )
    vec = jnp.moveaxis(vec.reshape(3, 4, 4, 64, 384), 2, 0).reshape(4, 3, 256, 384)
    got_x, tile, got_state = call(
        functools.partial(ring_kernel, "x"),
        (shape((4, 3, 256, 384)), shape((32, 128), f32), shape((3, 64, 384), f32)),
        [ANY, ANY],
        [VMEM, VMEM, ANY],
        [pltpu.VMEM((2, 3, 128, 384), bf16), pltpu.VMEM((32, 128), f32), pltpu.VMEM((16, 32, 128), f32)]
        + [DMA((6,)), DMA((6,)), DMA(())]
        + [DMA((15,))] * 2
        + [DMA((2,))] * 2,
        2,
    )(vec, state)
    coefs = tile_coefs(tile)
    vec = jnp.sum(got_x.astype(f32) * coefs[:, :, None, None], axis=0).astype(bf16)
    vec = jnp.moveaxis(vec.reshape(3, 4, 64, 384), 1, 0)
    got_y, tile = call(
        functools.partial(ring_kernel, "y"),
        (shape((4, 3, 64, 384)), shape((32, 128), f32)),
        [ANY],
        [VMEM, VMEM],
        [
            pltpu.VMEM((2, 3, 32, 384), bf16),
            pltpu.VMEM((32, 128), f32),
            pltpu.VMEM((16, 32, 128), f32),
            pltpu.VMEM((4, 32, 128), f32),
        ]
        + [DMA((6,)), DMA((6,)), DMA(())]
        + [DMA((15,))] * 2
        + [DMA((3,))] * 2,
        3,
    )(vec)
    coefs = tile_coefs(tile)
    part = jnp.sum(got_y.astype(f32) * coefs[:, :, None, None], axis=0)

    def adam(combined, weights, first, second):
        new_first = first_decay * first + (1.0 - first_decay) * combined
        new_second = second_decay * second + (1.0 - second_decay) * combined * combined
        first_hat = new_first / (1.0 - first_decay**adam_count)
        second_hat = new_second / (1.0 - second_decay**adam_count)
        new_weights = weights - learn_rate * (
            first_hat / (jnp.sqrt(second_hat) + adam_eps) + weight_decay * weights
        )
        return new_weights, new_first, new_second

    new_down = adam(part[2], got_state[0], got_state[1], got_state[2])[0].astype(bf16)
    returned, combined = call(
        final_kernel,
        (shape((8, 16, 2048)), shape((3, 32, 768), f32)),
        [ANY, ANY, VMEM],
        [ANY, ANY],
        [
            pltpu.VMEM((1, 4, 2, 4, 64, 384), bf16),
            pltpu.VMEM((2, 8, 16, 2048), f32),
            pltpu.VMEM((8, 16, 2048), f32),
            pltpu.VMEM((8, 16, 2048), bf16),
            DMA(()),
        ]
        + [DMA((GATHER_SEMS,))] * 2
        + [DMA((2,))] * 2
        + [DMA((8,))] * 4,
        4,
    )(new_down[None], part, hidden.reshape(2, 128, 384))
    pool_ids = jnp.arange(64, dtype=jnp.int32)
    selector = ((route[None, :] == pool_ids[:, None]) & live_slots[None, :]).astype(bf16)
    forward = jnp.dot(selector, returned.reshape(128, 2048), preferred_element_type=f32).astype(bf16)
    new_weights, new_first, new_second = adam(combined, masters, first_moment[0], second_moment[0])
    return (combined[None], new_weights[None], new_first[None], new_second[None], forward)


def solution(mesh):
    split = Mesh(mesh.devices.reshape(4, 8, 2, 4, 2), AXES)
    return jax.shard_map(
        shards,
        mesh=split,
        in_specs=(
            P(DP + EXPERT, None),
            P(DP + EXPERT, None),
            P(DP + EXPERT),
            P(DP + EXPERT, None),
            P(EXPERT, DP, None),
            P(EXPERT, DP, None),
            P(EXPERT, DP, None),
            P(EXPERT, None, DP, None),
            P(EXPERT, None, DP, None),
        ),
        out_specs=(
            P(EXPERT, None, DP, None),
            P(EXPERT, None, DP, None),
            P(EXPERT, None, DP, None),
            P(EXPERT, None, DP, None),
            P(DP + EXPERT, None),
        ),
        check_vma=False,
    )
```

time: 782 us -> 289 us (0.37)
  waiting for transfers between devices: 460 us -> 0 us
  Pallas kernels: 0 us -> 263 us
  starting transfers between devices: 157 us -> 0 us
  blocking collectives: 54.1 us -> 0 us
  local copies, waits for them, and re-layouts: 58.5 us -> 13.5 us
  other arithmetic: 24.9 us -> 5.26 us
  between operations: 14.8 us -> 1.13 us
    ppermute x31 -> x0, waiting for transfers between devices: 304 us -> none  [swapped(): lax.ppermute(array, axis, [(i, i ^ 1 << apart) for i in range(lax.axis_si...]
    pallas_call x0 -> x5, Pallas kernels: none -> 263 us  [the longest x1 92.5 us: shards(): call(dispatch_kernel, (shape((2, 8, 16, 2048)), shape((2, 8, 16, 2048)),...]
    all_gather x2 -> x0, waiting for transfers between devices: 150 us -> none  [all_blocks(): parts = lax.all_gather(parts, axes[k], axis=0, tiled=True)]
    ppermute x31 -> x0, starting transfers between devices: 147 us -> none  [swapped(): lax.ppermute(array, axis, [(i, i ^ 1 << apart) for i in range(lax.axis_si...]
    dynamic_slice x6 -> x0, local copies, waits for them, and re-layouts: 31.7 us -> none  [half_columns(): chosen = lax.dynamic_index_in_dim(shaped, selected, 2, keepdims=False)]
    all_to_all x2 -> x0, blocking collectives: 31.1 us -> none  [the longest x1 17.8 us: shards(): lax.all_to_all(sent_grads, EXPERT, split_axis=0, concat_axis=0, tiled=True)]
    all_gather x2 -> x0, blocking collectives: 22.9 us -> none  [all_blocks(): parts = lax.all_gather(parts, axes[k], axis=0, tiled=True)]
    reduce_sum x6 -> x2, other arithmetic: 12.1 us -> 0.73 us  [the longest x1 0.54 us: shards(): jnp.sum(got_x.astype(f32) * coefs[:, :, None, None], axis=0).astype(bf16)]
  transfers between devices with their start and end apart: 35 -> 0, of which waited for: 31 -> 0; matrix products, arithmetic and copies ran while one was open for 7% -> 0% of each run, Pallas kernels for 0% -> 0%
where the time goes in v1:
time: 289 us; the launch traced here: 288 us
  Pallas kernels  263 us (91%)
  local copies, waits for them, and re-layouts  13.5 us (5%)
  matrix products  5.5 us (2%)
  other arithmetic  5.26 us (2%)
    pallas_call x1, Pallas kernels, shards(): call(dispatch_kernel, (shape((2, 8, 16, 2048)), shape((2, 8, 16, 2048)),...  92.5 us
    pallas_call x1, Pallas kernels, shards(): call(final_kernel, (shape((8, 16, 2048)), shape((3, 32, 768), f32)), [ANY...  72.7 us
    pallas_call x1, Pallas kernels, shards(): call(functools.partial(ring_kernel, 'x'), (shape((4, 3, 256, 384)), shape...  41.4 us
    pallas_call x1, Pallas kernels, shards(): call(pair_kernel, (shape((4, 128, 1024)), shape((4, 128, 1024)), shape((3...  35.1 us
    pallas_call x1, Pallas kernels, shards(): call(functools.partial(ring_kernel, 'y'), (shape((4, 3, 64, 384)), shape(...  21.2 us

profile of v1, /device:TPU:7, one launch (start us, length us, event | category | flops | bytes accessed | tf_op | source)
XLA Modules:
  0.0 288.3 jit_solution(6188542616298452112)
XLA Ops:
  0.6 0.0 copy-start
  0.6 0.7 compare_select_fusion
  1.4 0.2 copy-done
  1.6 0.9 gather_fusion.1
  2.5 0.0 copy-done.14
  2.6 0.1 broadcast_in_dim.49
  2.6 0.1 reshape.1441
  2.7 0.0 copy-done.13
  2.7 0.9 gather_fusion
  3.7 0.0 copy-start.6
  3.7 0.0 copy-start.11
  3.7 0.0 copy-start.12
  3.7 0.2 select_select_fusion
  3.9 0.6 copy-done.6
  4.6 0.0 copy-done.11
  4.6 0.0 copy-done.12
  4.7 0.0 copy-start.9
  4.7 0.7 copy-done.9
  5.4 92.5 %shard_map.128 = (bf16[2,8,16,2048]{3,2,1,0:T(8,128)(2,1)S(1)}, bf16[2,8,16,2048]{3,2,1,0:T(8,128)(2,1)S(1)}, bf16[3,4,2,4,64,384]{5,4,3,2,1,0:T(8,128)(2,1)}, bf16[2,3,32,384]{3,2,1,0:T(8,128)(2,1)}) custom-call(bf16[8,16,2048]{2,1,0:T(8,128)(2,1)S(1)} %bitcast.609, bf16[8,16,2048]{2,1,0:T(8,128)(2,1)S(1)} %bitcast.608, ...), custom_call_target="tpu_custom_call" | custom-call | tf_op jit(solution)/shard_map/pallas_call | solution.py:550
  98.0 2.9 %fusion.112 = (bf16[1,4,2,4,64,384]{5,4,3,2,1,0:T(8,128)(2,1)S(1)}, bf16[1,4,2,4,64,384]{5,4,3,2,1,0:T(8,128)(2,1)S(1)}, bf16[1,4,2,4,64,384]{5,4,3,2,1,0:T(8,128)(2,1)S(1)}) fusion(bf16[3,4,2,4,64,384]{5,4,3,2,1,0:T(8,128)(2,1)} %get-tuple-element.23), kind=kLoop, calls=%fused_computation.222 | loop fusion | bytes 9437184 | tf_op jit(solution)/shard_map/slice | solution.py:568
  100.9 0.7 fusion.114
  101.6 0.7 fusion.115
  102.4 0.0 slice-start
  102.4 0.9 multiply_convert_fusion.3
  103.3 0.0 slice-start.1
  103.3 0.1 pad_maximum_fusion.1.hid
  103.4 0.0 slice-done
  103.4 0.1 stack.72
  103.5 0.7 slice-done.1
  104.2 0.1 stack.71
  104.3 35.1 %shard_map.129 = (bf16[4,128,1024]{2,1,0:T(8,128)(2,1)S(1)}, bf16[4,128,1024]{2,1,0:T(8,128)(2,1)S(1)}, bf16[3,4,128,384]{3,2,1,0:T(8,128)(2,1)}, f32[2,3,32,384]{3,2,1,0:T(8,128)S(1)}, f32[32,128]{1,0:T(8,128)S(1)}) custom-call(bf16[2,128,2048]{2,1,0:T(8,128)(2,1)S(1)} %bitcast.604, bf16[2,128,2048]{2,1,0:T(8,128)(2,1)S(1)} %bitcast.606, ...), custom_call_target="tpu_custom_call" | custom-call | tf_op jit(solution)/shard_map/pallas_call | solution.py:577
  139.4 1.0 copy-done.1
  140.4 1.0 copy-done.3
  141.4 0.1 slice_reduce_fusion.2
  141.5 0.1 reshape_squeeze.9
  141.6 0.3 slice_reduce_fusion.31
  142.0 0.1 copy.24
  142.1 1.7 multiply_convert_fusion
  143.8 0.1 fusion.113
  144.0 1.1 copy-done.4
  145.0 0.7 convolution_convert_fusion.1
  145.8 0.7 convolution_convert_fusion.2
  146.6 0.7 convolution_convert_fusion.3
  147.3 0.3 pad_maximum_fusion
  147.6 0.3 copy.29
  147.9 41.4 %shard_map.130 = (bf16[4,3,256,384]{3,2,1,0:T(8,128)(2,1)S(1)}, f32[32,128]{1,0:T(8,128)S(1)}, f32[3,64,384]{2,1,0:T(8,128)S(1)}) custom-call(bf16[4,3,256,384]{3,2,1,0:T(8,128)(2,1)S(1)} %bitcast.601, f32[2,3,32,384]{3,2,1,0:T(8,128)S(1)} %get-tuple-element.28.refs_1_), custom_call_target="tpu_custom_call" | custom-call | tf_op jit(solution)/shard_map/pallas_call | solution.py:608
  189.3 0.1 slice_reduce_fusion.1
  189.5 0.1 reshape_squeeze.10
  189.5 0.3 slice_reduce_fusion.21
  190.0 0.5 multiply_reduce_fusion
  190.5 0.1 copy.39
  190.6 0.0 copy-start.10
  190.6 0.0 copy-start.7
  190.6 0.0 copy-start.8
  190.6 21.2 %shard_map.131 = (bf16[4,3,64,384]{3,2,1,0:T(8,128)(2,1)S(1)}, f32[32,128]{1,0:T(8,128)S(1)}) custom-call(bf16[4,3,64,384]{3,2,1,0:T(8,128)(2,1)S(1)} %bitcast.607), custom_call_target="tpu_custom_call" | custom-call | tf_op jit(solution)/shard_map/pallas_call | solution.py:622
  211.8 0.1 slice_reduce_fusion
  211.9 0.1 reshape_squeeze.11
  212.0 0.3 slice_reduce_fusion.11
  212.5 0.2 multiply_reduce_fusion.1.comb
  212.7 0.1 subtract_convert_fusion.mine
  212.8 72.7 %shard_map.132 = (bf16[8,16,2048]{2,1,0:T(8,128)(2,1)S(1)}, f32[3,32,768]{2,1,0:T(8,128)S(1)}) custom-call(bf16[1,64,384]{2,1,0:T(8,128)(2,1)S(1)} %subtract_convert_fusion.mine, f32[3,64,384]{2,1,0:T(8,128)S(1)} %multiply_reduce_fusion.1.comb, bf16[2,128,384]{2,1,0:T(8,128)(2,1)S(1)} %bitcast.612), custom_call_target="tpu_custom_call" | custom-call | tf_op jit(solution)/shard_map/pallas_call | solution.py:652
  285.5 1.1 fusion.9
  286.6 0.9 convolution_convert_fusion
  287.5 0.7 copy.45
  (39 shorter events, 0.4 us)
Async XLA Ops:
  0.6 1.0 copy-start
  1.6 0.9 copy-start.14
  1.6 1.1 copy-start.13
  1.6 1.1 copy-start.5
  3.7 0.9 copy-start.6
  3.7 0.9 copy-start.11
  3.7 1.0 copy-start.12
  4.7 0.7 copy-start.9
  102.4 1.0 slice-start
  103.3 0.9 slice-start.1
  139.4 1.0 copy-start.1
  140.4 1.0 copy-start.3
  143.8 1.2 copy-start.4
  144.0 1.8 copy-start.2
  190.6 94.8 %copy-start.10 = (f32[3,32,768]{2,1,0:T(8,128)S(1)}, f32[3,32,768]{2,1,0:T(8,128)}, u32[]{:S(2)}) copy-start(f32[3,32,768]{2,1,0:T(8,128)} %copy-done.9) | copy-start | bytes 884740
  190.6 94.9 %copy-start.7 = (f32[1,3,32,768]{3,2,1,0:T(8,128)S(1)}, f32[1,3,32,768]{3,2,1,0:T(8,128)}, u32[]{:S(2)}) copy-start(f32[1,3,32,768]{3,2,1,0:T(8,128)} %param.19) | copy-start | bytes 884740
  190.6 94.9 %copy-start.8 = (f32[1,3,32,768]{3,2,1,0:T(8,128)S(1)}, f32[1,3,32,768]{3,2,1,0:T(8,128)}, u32[]{:S(2)}) copy-start(f32[1,3,32,768]{3,2,1,0:T(8,128)} %param.18) | copy-start | bytes 884740

commit v2 on v1

v2 whole, which is shorter than its diff:
```python
import jax
import jax.numpy as jnp
from jax import lax
from jax.experimental import pallas as pl
from jax.experimental.pallas import tpu as pltpu
from jax.sharding import Mesh
from jax.sharding import PartitionSpec as P

AXES = ("y", "t", "l", "x", "c")
DP = ("y", "t", "l")
EXPERT = ("x", "c")
MESH_ID = pl.DeviceIdType.MESH

first_decay = 0.9
second_decay = 0.95
learn_rate = 0.01
adam_eps = 1e-08
weight_decay = 0.1
adam_count = 100.0
norm_eps = 1e-06
ANY = pl.BlockSpec(memory_space=pl.ANY)
VMEM = pl.BlockSpec(memory_space=pltpu.VMEM)
DMA = pltpu.SemaphoreType.DMA


def place():
    return tuple(lax.axis_index(a) for a in AXES)


def remote(src, dst, send_sem, recv_sem, dev):
    return pltpu.make_async_remote_copy(
        src_ref=src,
        dst_ref=dst,
        send_sem=send_sem,
        recv_sem=recv_sem,
        device_id=dev,
        device_id_type=MESH_ID,
    )


def full(dev):
    return {a: dev[a] if a in dev else lax.axis_index(a) for a in AXES}


def is_self(dev):
    same = None
    for a in AXES:
        if a in dev:
            eq = lax.axis_index(a) == dev[a]
            same = eq if same is None else jnp.logical_and(same, eq)
    return same


def greet(others, maybe_self):
    barrier = pltpu.get_barrier_semaphore()
    for dev in others:
        pl.semaphore_signal(barrier, inc=1, device_id=dev, device_id_type=MESH_ID)
    for dev in maybe_self:
        pl.semaphore_signal(barrier, inc=1, device_id=dev, device_id_type=MESH_ID)
    pl.semaphore_wait(barrier, len(others) + len(maybe_self))


def send_or_copy(src, dst, send_sem, recv_sem, dev):
    mine = is_self(dev)

    @pl.when(mine)
    def _():
        pltpu.make_async_copy(src, dst, recv_sem).start()

    @pl.when(jnp.logical_not(mine))
    def _():
        remote(src, dst, send_sem, recv_sem, dev).start()


def wait_sent(src, dst, send_sem, recv_sem, dev):
    @pl.when(jnp.logical_not(is_self(dev)))
    def _():
        remote(src, dst, send_sem, recv_sem, dev).wait_send()


def landed(ref, recv_sem):
    pltpu.make_async_copy(ref, ref, recv_sem).wait()


def worker_of_rows(e):
    y, t, l, x, c = place()
    return {"t": e, "l": t % 2, "x": (t // 2 + e) % 4, "c": l}


def tree_place(x, t):
    return (x + 8 - t) % 4


def source_of_rows(s):
    y, t, l, x, c = place()
    return {"t": 2 * tree_place(x, t) + l, "l": c, "x": s // 2, "c": s % 2}


def row_x(x, t):
    return (x + 8 - t // 2 - 2 * (t % 2)) % 4


def relay_shift():
    t, c = lax.axis_index("t"), lax.axis_index("c")
    return (t + 2 * c) % 4


def relay_to():
    return {"x": (lax.axis_index("x") + relay_shift()) % 4}


def relay_from():
    return {"x": (lax.axis_index("x") + 4 - relay_shift()) % 4}


def block_expert():
    return 2 * relay_from()["x"] + lax.axis_index("c")


def worker_of_block(h):
    return {"t": block_expert(), "l": lax.axis_index("t") // 4, "c": h}


def sender_of_block(k):
    y, t, l, x, c = place()
    return {"t": 4 * l + row_x(x, t), "l": k, "c": t % 2}


def block_of_owner(h):
    y, t, l, x, c = place()
    return {"t": 2 * x + c, "l": t // 4, "x": relay_to()["x"], "c": h}


def owner_of_block(k):
    y, t, l, x, c = place()
    return {"t": 4 * l + row_x(x, t), "l": k, "x": t // 2, "c": t % 2}


def ring(axis, step):
    return {axis: (lax.axis_index(axis) + step) % 4}


def gather_peers():
    l = lax.axis_index("l")
    return [{"l": 1 - l}, ring("x", 1), ring("x", 3), ring("y", 1), ring("y", 3)]


def gather_swap(g, send, recv):
    y, t, l, x, c = place()
    mine = g.at[:, y, l, row_x(x, t)]
    swap = remote(mine, mine, send.at[0], recv.at[0], {"l": 1 - l})
    swap.start()
    return swap


def gather_steps(g, swap, send, recv):
    y, t, l, x, c = place()
    rows = g.shape[4] // 2
    first, last = pl.ds(0, rows), pl.ds(rows, rows)
    swap.wait_send()
    landed(g.at[:, y, 1 - l, row_x(x, t)], recv.at[0])

    def start_ring(axis, parts, base):
        at = lax.axis_index(axis)
        for k, step in ((0, 1), (1, 3)):
            part = parts(at, 0, 2)
            remote(part, part, send.at[base + k], recv.at[base + k], ring(axis, step)).start()

    def relay_ring(axis, parts, base):
        at = lax.axis_index(axis)
        for k, step in ((0, 1), (1, 3)):
            came = (at + 4 - step) % 4
            landed(parts(came, 0, 2), recv.at[base + k])
            part = parts(came, k, 1)
            remote(part, part, send.at[base + 2 + k], recv.at[base + 2 + k], ring(axis, step)).start()

    def end_ring(axis, parts, base):
        at = lax.axis_index(axis)
        for k, step in ((0, 1), (1, 3)):
            part = parts(at, 0, 2)
            remote(part, part, send.at[base + k], recv.at[base + k], ring(axis, step)).wait_send()
            part = parts((at + 4 - step) % 4, k, 1)
            remote(part, part, send.at[base + 2 + k], recv.at[base + 2 + k], ring(axis, step)).wait_send()
            landed(parts((at + 2) % 4, k, 1), recv.at[base + 2 + k])

    def x_one(at, k, n):
        return g.at[:, y, pl.ds(k, n), row_x(at, t), first]

    def y_one(at, k, n):
        return g.at[:, at, pl.ds(k, n), row_x(x, t), last]

    def y_all(at, k, n):
        return g.at[:, at, pl.ds(k, n), :, first]

    def x_all(at, k, n):
        return g.at[:, :, pl.ds(k, n), row_x(at, t), last]

    for one, two, base in ((("x", x_one), ("y", y_one), 1), (("y", y_all), ("x", x_all), 9)):
        start_ring(*one, base)
        start_ring(*two, base + 4)
        yield
        relay_ring(*one, base)
        relay_ring(*two, base + 4)
        yield
        end_ring(*one, base)
        end_ring(*two, base + 4)
        yield


def gather_block(g, swap, send, recv):
    for _ in gather_steps(g, swap, send, recv):
        pass


GATHER_SEMS = 17


EARLY = 4


def dispatch_kernel(
    tok, grd, wts, xt, xg, g, relay, xpt, xpg,
    s_row, r_row, s_fwd, r_fwd, s_rl, r_rl, s_wt, r_wt, s_g, r_g, s_x, r_x, s_xf, r_xf,
):
    y, t, l, x, c = place()
    other, across = {"c": 1 - c}, {"l": 1 - l}
    greet(
        [other] + gather_peers(),
        [worker_of_rows(e) for e in range(8)]
        + [source_of_rows(s) for s in range(8)]
        + [worker_of_block(h) for h in range(2)]
        + [sender_of_block(k) for k in range(2)]
        + [relay_to(), relay_from()],
    )
    to_relay = (wts, relay, s_rl, r_rl, relay_to())
    send_or_copy(*to_relay)
    row_sends = []
    slot = 2 * x + c
    for src, dst, which in ((tok, xt, 0), (grd, xg, 1)):
        for k, off in enumerate((4, 2, 6, 1, 7, 3, 5, 0)):
            e = (t + off) % 8
            row_sends.append(
                (src.at[e], dst.at[l, slot], s_row.at[which, k], r_row.at[which, slot], worker_of_rows(e))
            )
    for a in row_sends[:EARLY]:
        send_or_copy(*a)
    landed(relay, r_rl)
    chunk = g.at[:, y, t // 4, t % 4, pl.ds(pl.multiple_of(l * 32, 32), 32)]
    weight_sends = [(relay.at[h], chunk, s_wt.at[h], r_wt.at[l], worker_of_block(h)) for h in range(2)]
    for a in weight_sends:
        send_or_copy(*a)
    mine = g.at[:, y, l, row_x(x, t)]
    for k in range(2):
        landed(mine.at[:, pl.ds(32 * k, 32)], r_wt.at[k])
    swap = gather_swap(g, s_g, r_g)
    for a in row_sends[EARLY:8]:
        send_or_copy(*a)
    steps = gather_steps(g, swap, s_g, r_g)
    for _ in range(3):
        next(steps)
    for a in row_sends[8:]:
        send_or_copy(*a)
    next(steps)
    forwards, crossings = [], []

    def rows_in(dst, far, which):
        for s in range(8):
            part = dst.at[c, s]
            landed(part, r_row.at[which, s])
            f = remote(part, part, s_fwd.at[which, s], r_fwd.at[which, s], other)
            f.start()
            forwards.append(f)
        for n in range(4):
            cols = pl.ds(pl.multiple_of(512 * n + (1 - l) * 256, 256), 256)
            f = remote(
                dst.at[c, :, :, cols],
                far.at[c, :, :, pl.ds(256 * n, 256)],
                s_x.at[which, n],
                r_x.at[which, n],
                across,
            )
            f.start()
            crossings.append(f)

    def crossed(far, which):
        for n in range(4):
            piece = far.at[c, :, :, pl.ds(256 * n, 256)]
            landed(piece, r_x.at[which, n])
            f = remote(piece, piece, s_xf.at[which, n], r_xf.at[which, n], other)
            f.start()
            forwards.append(f)

    rows_in(xt, xpt, 0)
    next(steps)
    crossed(xpt, 0)
    rows_in(xg, xpg, 1)
    next(steps)
    for a in [to_relay] + weight_sends + row_sends:
        wait_sent(*a)
    crossed(xpg, 1)
    for f in forwards + crossings:
        f.wait_send()
    for dst, far, which in ((xt, xpt, 0), (xg, xpg, 1)):
        for s in range(8):
            landed(dst.at[1 - c, s], r_fwd.at[which, s])
        for n in range(4):
            landed(far.at[1 - c, :, :, pl.ds(256 * n, 256)], r_xf.at[which, n])


PAIRS = [(i, k) for i in range(4) for k in range(i, 4)]
LAST = (((1,), (1,)), ((), ()))


def small_peers(with_x):
    y, t, l, x, c = place()
    out = []
    for dx in range(4 if with_x else 1):
        for dl in range(2):
            for dc in range(2):
                if dx + dl + dc > 0:
                    out.append({"x": (x + dx) % 4, "l": (l + dl) % 2, "c": (c + dc) % 2})
    return out


def small_sum(part, box, peers, at, send, recv):
    box[at] = part
    sends = []
    for k, dev in enumerate(peers):
        f = remote(box.at[at], box.at[at], send.at[k], recv.at[k], dev)
        f.start()
        sends.append(f)
    for k in range(len(peers)):
        landed(box.at[at], recv.at[k])
    for f in sends:
        f.wait_send()
    return jnp.sum(box[...], axis=0)


def gram_tile(r, lines):
    rows = r.shape[2]
    lines[...] = jnp.zeros_like(lines)
    for m in range(3):

        def step(i, accs, m=m):
            at = pl.ds(pl.multiple_of(i * 16, 16), 16)
            parts = [r[k, m, at, :].astype(jnp.float32) for k in range(4)]
            out = []
            for n, (i1, i2) in enumerate(PAIRS):
                prod = parts[i1] * parts[i2]
                out.append(accs[n] + (prod[:8] + prod[8:]))
            return tuple(out)

        zero = tuple(jnp.zeros((8, 384), jnp.float32) for _ in PAIRS)
        accs = lax.fori_loop(0, rows // 16, step, zero)
        for n, acc in enumerate(accs):
            line = jnp.sum(acc, axis=0, keepdims=True)
            lines[pl.ds(10 * m + n, 1), :] = line[:, :128] + line[:, 128:256] + line[:, 256:]
    return jnp.broadcast_to(jnp.sum(lines[...], axis=1, keepdims=True), (32, 128))


def pair_coefs(cross, lower, upper):
    return (
        1.0 - cross / (2.0 * (lower + norm_eps)),
        1.0 - cross / (2.0 * (upper + norm_eps)),
    )


def quad_coefs(gram):
    a0, b0 = pair_coefs(gram[0][1], gram[0][0], gram[1][1])
    a1, b1 = pair_coefs(gram[2][3], gram[2][2], gram[3][3])
    lower = a0 * a0 * gram[0][0] + 2.0 * a0 * b0 * gram[0][1] + b0 * b0 * gram[1][1]
    upper = a1 * a1 * gram[2][2] + 2.0 * a1 * b1 * gram[2][3] + b1 * b1 * gram[3][3]
    cross = a0 * (a1 * gram[0][2] + b1 * gram[0][3]) + b0 * (a1 * gram[1][2] + b1 * gram[1][3])
    a2, b2 = pair_coefs(cross, lower, upper)
    return [a2 * a0, a2 * b0, b2 * a1, b2 * b1]


def tile_coefs(tile, m):
    gram = [[None] * 4 for _ in range(4)]
    for n, (i, k) in enumerate(PAIRS):
        gram[i][k] = tile[10 * m + n : 10 * m + n + 1, :]
    return [jnp.concatenate([w, w, w], axis=1) for w in quad_coefs(gram)]


def ring_exchange(axis, v, r, relay, part, slot, sv, rv, own):
    at = lax.axis_index(axis)
    rows = r.shape[2]
    up, down = ring(axis, 1), ring(axis, 3)
    low, high = pl.ds(0, rows // 2), pl.ds(rows // 2, rows // 2)
    far, nxt, prv = (at + 2) % 4, (at + 1) % 4, (at + 3) % 4
    first = [
        remote(v.at[part(far), :, low], relay.at[0], sv.at[0], rv.at[0], up),
        remote(v.at[part(far), :, high], relay.at[1], sv.at[1], rv.at[1], down),
        remote(v.at[part(nxt)], r.at[slot(at)], sv.at[2], rv.at[2], up),
        remote(v.at[part(prv)], r.at[slot(at)], sv.at[3], rv.at[3], down),
    ]
    for f in first:
        f.start()
    keep = pltpu.make_async_copy(v.at[part(at)], r.at[slot(at)], own)
    keep.start()
    landed(relay.at[0], rv.at[0])
    fwd_up = remote(relay.at[0], r.at[slot(prv), :, low], sv.at[4], rv.at[4], up)
    fwd_up.start()
    landed(relay.at[1], rv.at[1])
    fwd_down = remote(relay.at[1], r.at[slot(nxt), :, high], sv.at[5], rv.at[5], down)
    fwd_down.start()
    keep.wait()
    landed(r.at[slot(prv)], rv.at[2])
    landed(r.at[slot(nxt)], rv.at[3])
    landed(r.at[slot(far), :, low], rv.at[4])
    landed(r.at[slot(far), :, high], rv.at[5])
    for f in first + [fwd_up, fwd_down]:
        f.wait_send()


def adam(combined, weights, first, second):
    new_first = first_decay * first + (1.0 - first_decay) * combined
    new_second = second_decay * second + (1.0 - second_decay) * combined * combined
    first_hat = new_first / (1.0 - first_decay**adam_count)
    second_hat = new_second / (1.0 - second_decay**adam_count)
    new_weights = weights - learn_rate * (
        first_hat / (jnp.sqrt(second_hat) + adam_eps) + weight_decay * weights
    )
    return new_weights, new_first, new_second


def tree_kernel(
    xt, xg, xpt, xpg, hid, master, moment1, moment2,
    ret, got,
    ft, fg, fh, fs, gram, lines, relay, own_state, v, r, rel, vy, ry, rely, comb, g, part, came, rounded, via,
    box_a, box_b, box_c, box_d,
    own, s_h, r_h, s_rl, r_rl, s_st, r_st, sv, rv, sw, rw,
    s_a, r_a, s_b, r_b, s_c, r_c, s_d, r_d, s_g, r_g, s_o, r_o, s_p, r_p, s_y, r_y, s_z, r_z,
):
    y, t, l, x, c = place()
    across, other = {"l": 1 - l}, {"c": 1 - c}
    quad, wide = small_peers(False), small_peers(True)
    column = [ring("y", k) for k in range(1, 4)]
    row_home = [{"t": 2 * q + l, "l": k} for q in range(4) for k in range(2)]
    row_from = [{"t": e, "l": t % 2} for e in range(8)]
    row_via = [{"x": s // 2, "c": s % 2} for s in range(8)]
    mine = 2 * l
    theirs = 2 * (1 - l)
    local = [pltpu.make_async_copy(hid, fh.at[:, pl.ds(mine, 2)], own.at[8])]
    for k, (src, far, dst) in enumerate(((xt, xpt, ft), (xg, xpg, fg))):
        for n in range(4):
            cols = pl.ds(pl.multiple_of(512 * n + l * 256, 256), 256)
            local.append(
                pltpu.make_async_copy(
                    src.at[:, :, cols], dst.at[pl.ds(mine, 2), :, pl.ds(256 * n, 256)], own.at[4 * k + n]
                )
            )
        local.append(pltpu.make_async_copy(far, dst.at[pl.ds(theirs, 2)], own.at[9 + k]))
    for f in local:
        f.start()
    greet(
        quad + wide + column,
        [worker_of_block(h) for h in range(2)]
        + [sender_of_block(k) for k in range(2)]
        + [block_of_owner(h) for h in range(2)]
        + [owner_of_block(k) for k in range(2)]
        + [relay_to(), relay_from()]
        + row_home
        + row_from,
    )
    cross = remote(hid, fh.at[:, pl.ds(mine, 2)], s_h, r_h, across)
    cross.start()
    to_relay = [
        (src, relay.at[k], s_rl.at[k], r_rl.at[k], relay_to())
        for k, src in enumerate((master.at[0], moment1.at[0, 2], moment2.at[0, 2]))
    ]
    for a in to_relay:
        send_or_copy(*a)
    for f in local:
        f.wait()
    for k in range(3):
        landed(relay.at[k], r_rl.at[k])
    piece = pl.ds(pl.multiple_of(l * 32, 32), 32)
    state_sends = [
        (relay.at[:, :, pl.ds(384 * h, 384)], own_state.at[:, piece], s_st.at[h], r_st.at[l], worker_of_block(h)) for h in range(2)
    ]
    for a in state_sends:
        send_or_copy(*a)

    for n, (i, k) in enumerate(PAIRS):
        gram[0, n] = lax.dot_general(ft[i], ft[k], LAST, preferred_element_type=jnp.float32)
        gram[1, n] = lax.dot_general(fg[i], fg[k], LAST, preferred_element_type=jnp.float32)
    landed(fh.at[:, pl.ds(theirs, 2)], r_h)
    lines[...] = jnp.zeros_like(lines)
    for n, (i, k) in enumerate(PAIRS):
        for m in range(3):
            inner = lax.dot_general(fh[m, i], fh[m, k], LAST, preferred_element_type=jnp.float32)
            lines[pl.ds(10 * m + n, 1), :] = jnp.sum(gram[m // 2, n] * inner, axis=0, keepdims=True)
    total = jnp.broadcast_to(jnp.sum(lines[...], axis=1, keepdims=True), (32, 128))
    total = small_sum(total, box_a, quad, 2 * l + c, s_a, r_a)
    for m in range(3):
        for k, w in enumerate(tile_coefs(total, m)):
            fs[m, pl.ds(128 * k, 128), :] = (fh[m, k].astype(jnp.float32) * w).astype(jnp.bfloat16)
    for src, matrices in ((ft, (0, 1)), (fg, (2,))):
        for n in range(4):
            cols = src[:, :, pl.ds(256 * n, 256)].reshape(512, 256)
            for m in matrices:
                block = lax.dot_general(
                    cols, fs[m], (((0,), (0,)), ((), ())), preferred_element_type=jnp.float32
                ).astype(jnp.bfloat16)
                for q in range(4):
                    v[q, m, pl.ds(64 * n, 64), :] = block[64 * q : 64 * q + 64]

    ring_exchange("x", v, r, rel, lambda p: row_x(p, t), lambda p: tree_place(p, t), sv, rv, own.at[0])
    total = small_sum(gram_tile(r, lines), box_b, wide, x * 4 + l * 2 + c, s_b, r_b)
    for m in range(3):
        w = tile_coefs(total, m)
        for n in range(4):
            acc = r[0, m, pl.ds(64 * n, 64), :].astype(jnp.float32) * w[0]
            for k in range(1, 4):
                acc = acc + r[k, m, pl.ds(64 * n, 64), :].astype(jnp.float32) * w[k]
            vy[n, m] = acc.astype(jnp.bfloat16)

    ring_exchange("y", vy, ry, rely, lambda p: p, lambda p: p, sw, rw, own.at[1])
    total = small_sum(gram_tile(ry, lines), box_c, wide, x * 4 + l * 2 + c, s_c, r_c)
    total = small_sum(total, box_d, column, y, s_d, r_d)
    for k in range(2):
        landed(own_state.at[:, pl.ds(32 * k, 32)], r_st.at[k])
    for m in range(3):
        w = tile_coefs(total, m)
        acc = ry[0, m].astype(jnp.float32) * w[0]
        for k in range(1, 4):
            acc = acc + ry[k, m].astype(jnp.float32) * w[k]
        comb[m] = acc
    g[0, y, l, row_x(x, t)] = adam(comb[2], own_state[0], own_state[1], own_state[2])[0].astype(jnp.bfloat16)

    swap = gather_swap(g, s_g, r_g)
    half = pl.ds(pl.multiple_of(c * 384, 384), 384)
    owner_sends = [
        (comb.at[:, pl.ds(32 * k, 32)], got.at[:, :, half], s_o.at[k], r_o.at[c], owner_of_block(k)) for k in range(2)
    ]
    for a in owner_sends:
        send_or_copy(*a)
    gather_block(g, swap, s_g, r_g)
    for n in range(8):
        rows = g[0, n // 2, n % 2].reshape(256, 384)
        for k in range(2):
            block = lax.dot_general(fh[2, mine + k], rows, LAST, preferred_element_type=jnp.float32)
            part[k, :, :, pl.ds(256 * n, 256)] = block.reshape(8, 16, 256)
    swaps = []
    for s in range(8):
        f = remote(part.at[1 - c, s], came.at[s], s_p.at[s], r_p.at[s], other)
        f.start()
        swaps.append(f)
    backs = []
    slot = 2 * tree_place(x, t) + c
    for s in range(8):
        landed(came.at[s], r_p.at[s])
        rounded[s] = (part[c, s] + came[s]).astype(jnp.bfloat16)
        a = (rounded.at[s], via.at[slot], s_y.at[s], r_y.at[slot], row_via[s])
        send_or_copy(*a)
        backs.append(a)
    for q in range(8):
        landed(via.at[q], r_y.at[q])
        a = (via.at[q], ret.at[t], s_z.at[q], r_z.at[t], row_home[q])
        send_or_copy(*a)
        backs.append(a)
    cross.wait_send()
    for f in swaps:
        f.wait_send()
    for a in to_relay + state_sends + owner_sends + backs:
        wait_sent(*a)
    for h in range(2):
        landed(got.at[:, :, pl.ds(384 * h, 384)], r_o.at[h])
    for e in range(8):
        landed(ret.at[e], r_z.at[e])


def call(kernel, outs, in_specs, out_specs, scratch, cid):
    return pl.pallas_call(
        kernel,
        out_shape=outs,
        in_specs=in_specs,
        out_specs=out_specs,
        scratch_shapes=scratch,
        compiler_params=pltpu.CompilerParams(
            collective_id=cid, has_side_effects=True, vmem_limit_bytes=48 * 1024 * 1024
        ),
    )


def shape(dims, kind=jnp.bfloat16):
    return jax.ShapeDtypeStruct(dims, kind)


def shards(
    tokens,
    cotangent,
    route,
    counts,
    gate_master,
    up_master,
    down_master,
    first_moment,
    second_moment,
):
    y, t, l, x, c = place()
    bf16, f32 = jnp.bfloat16, jnp.float32
    slot_ids = jnp.arange(128, dtype=jnp.int32)
    live_slots = slot_ids % 16 < jnp.repeat(counts[0], 16)
    sent_tokens = jnp.where(live_slots[:, None], jnp.take(tokens, route, axis=0), 0)
    sent_grads = jnp.where(live_slots[:, None], jnp.take(cotangent, route, axis=0), 0)
    masters = jnp.stack([gate_master[0], up_master[0], down_master[0]])
    halves = jnp.moveaxis(masters.astype(bf16).reshape(3, 32, 2, 384), 2, 0)
    xt, xg, weights, _, xpt, xpg = call(
        dispatch_kernel,
        (
            shape((2, 8, 16, 2048)),
            shape((2, 8, 16, 2048)),
            shape((3, 4, 2, 4, 64, 384)),
            shape((2, 3, 32, 384)),
            shape((2, 8, 16, 1024)),
            shape((2, 8, 16, 1024)),
        ),
        [ANY] * 3,
        [ANY] * 6,
        [DMA((2, 8))] * 4 + [DMA(())] * 2 + [DMA((2,))] * 2 + [DMA((GATHER_SEMS,))] * 2 + [DMA((2, 4))] * 4,
        0,
    )(sent_tokens.reshape(8, 16, 2048), sent_grads.reshape(8, 16, 2048), halves)
    xt = xt.reshape(256, 2048)
    xg = xg.reshape(256, 2048)
    weights = weights.reshape(3, 2048, 384)
    gate_pre = jnp.dot(xt, weights[0], preferred_element_type=f32)
    up_pre = jnp.dot(xt, weights[1], preferred_element_type=f32)
    back_hidden = jnp.dot(xg, weights[2], preferred_element_type=f32)
    sigmoid_gate = jax.nn.sigmoid(gate_pre)
    active_gate = gate_pre * sigmoid_gate
    hidden = (active_gate * up_pre).astype(bf16)
    d_gate = (back_hidden * up_pre * sigmoid_gate * (1.0 + gate_pre * (1.0 - sigmoid_gate))).astype(bf16)
    d_up = (back_hidden * active_gate).astype(bf16)
    factors = jnp.stack([d_gate, d_up, hidden]).reshape(3, 2, 128, 384)
    box = pltpu.VMEM((16, 32, 128), f32)
    returned, combined = call(
        tree_kernel,
        (shape((8, 16, 2048)), shape((3, 32, 768), f32)),
        [ANY] * 8,
        [ANY] * 2,
        [
            pltpu.VMEM((4, 128, 1024), bf16),
            pltpu.VMEM((4, 128, 1024), bf16),
            pltpu.VMEM((3, 4, 128, 384), bf16),
            pltpu.VMEM((3, 512, 384), bf16),
            pltpu.VMEM((2, 10, 128, 128), f32),
            pltpu.VMEM((32, 128), f32),
            pltpu.VMEM((3, 32, 768), f32),
            pltpu.VMEM((3, 64, 384), f32),
            pltpu.VMEM((4, 3, 256, 384), bf16),
            pltpu.VMEM((4, 3, 256, 384), bf16),
            pltpu.VMEM((2, 3, 128, 384), bf16),
            pltpu.VMEM((4, 3, 64, 384), bf16),
            pltpu.VMEM((4, 3, 64, 384), bf16),
            pltpu.VMEM((2, 3, 32, 384), bf16),
            pltpu.VMEM((3, 64, 384), f32),
            pltpu.VMEM((1, 4, 2, 4, 64, 384), bf16),
            pltpu.VMEM((2, 8, 16, 2048), f32),
            pltpu.VMEM((8, 16, 2048), f32),
            pltpu.VMEM((8, 16, 2048), bf16),
            pltpu.VMEM((8, 16, 2048), bf16),
            pltpu.VMEM((4, 32, 128), f32),
            box,
            box,
            pltpu.VMEM((4, 32, 128), f32),
            DMA((11,)),
        ]
        + [DMA(())] * 2
        + [DMA((3,))] * 2
        + [DMA((2,))] * 2
        + [DMA((6,))] * 4
        + [DMA((3,))] * 2
        + [DMA((15,))] * 4
        + [DMA((3,))] * 2
        + [DMA((GATHER_SEMS,))] * 2
        + [DMA((2,))] * 2
        + [DMA((8,))] * 6,
        1,
    )(
        xt.reshape(2, 128, 2048),
        xg.reshape(2, 128, 2048),
        xpt.reshape(2, 128, 1024),
        xpg.reshape(2, 128, 1024),
        factors,
        down_master,
        first_moment,
        second_moment,
    )
    pool_ids = jnp.arange(64, dtype=jnp.int32)
    selector = ((route[None, :] == pool_ids[:, None]) & live_slots[None, :]).astype(bf16)
    forward = jnp.dot(selector, returned.reshape(128, 2048), preferred_element_type=f32).astype(bf16)
    new_weights, new_first, new_second = adam(combined, masters, first_moment[0], second_moment[0])
    return (combined[None], new_weights[None], new_first[None], new_second[None], forward)


def solution(mesh):
    split = Mesh(mesh.devices.reshape(4, 8, 2, 4, 2), AXES)
    return jax.shard_map(
        shards,
        mesh=split,
        in_specs=(
            P(DP + EXPERT, None),
            P(DP + EXPERT, None),
            P(DP + EXPERT),
            P(DP + EXPERT, None),
            P(EXPERT, DP, None),
            P(EXPERT, DP, None),
            P(EXPERT, DP, None),
            P(EXPERT, None, DP, None),
            P(EXPERT, None, DP, None),
        ),
        out_specs=(
            P(EXPERT, None, DP, None),
            P(EXPERT, None, DP, None),
            P(EXPERT, None, DP, None),
            P(EXPERT, None, DP, None),
            P(DP + EXPERT, None),
        ),
        check_vma=False,
    )
```

time: 289 us -> 273 us (0.945)
  the two profiles are of different devices: /device:TPU:7 before, /device:TPU:33 now
where the time goes in v2:
time: 273 us; the launch traced here: 272 us
  Pallas kernels  256 us (94%)
  local copies, waits for them, and re-layouts  6.64 us (2%)
  other arithmetic  5.77 us (2%)
  matrix products  3.2 us (1%)
    pallas_call x1, Pallas kernels, shards(): call(tree_kernel, (shape((8, 16, 2048)), shape((3, 32, 768), f32)), [ANY]...  159 us
    pallas_call x1, Pallas kernels, shards(): call(dispatch_kernel, (shape((2, 8, 16, 2048)), shape((2, 8, 16, 2048)),...  96.7 us

profile of v2, /device:TPU:33, one launch (start us, length us, event | category | flops | bytes accessed | tf_op | source)
XLA Modules:
  0.0 272.5 jit_solution(11371043125529689866)
XLA Ops:
  0.6 0.0 copy-start
  0.6 0.7 compare_select_fusion
  1.4 0.7 broadcast_in_dim.45
  2.1 0.1 reshape.93
  2.2 0.7 compare_and_fusion
  2.8 1.0 constant_dynamic-update-slice_fusion.2
  3.8 1.0 constant_dynamic-update-slice_fusion.1
  4.8 1.0 constant_dynamic-update-slice_fusion
  5.8 0.0 copy-done
  5.9 0.0 copy-start.4
  5.9 0.9 gather_fusion.1
  6.8 0.0 copy-done.4
  6.8 0.9 gather_fusion
  7.8 0.2 select_select_fusion
  8.0 96.7 %shard_map.128 = (bf16[2,8,16,2048]{3,2,1,0:T(8,128)(2,1)S(1)}, bf16[2,8,16,2048]{3,2,1,0:T(8,128)(2,1)S(1)}, bf16[3,4,2,4,64,384]{5,4,3,2,1,0:T(8,128)(2,1)}, b...) custom-call(bf16[8,16,2048]{2,1,0:T(8,128)(2,1)S(1)} %bitcast.60, ...), custom_call_target="tpu_custom_call" | custom-call | tf_op jit(solution)/shard_map/pallas_call | solution.py:610
  104.7 3.1 %fusion.9 = (bf16[1,4,2,4,64,384]{5,4,3,2,1,0:T(8,128)(2,1)S(1)}, bf16[1,4,2,4,64,384]{5,4,3,2,1,0:T(8,128)(2,1)S(1)}, bf16[1,4,2,4,64,384]{5,4,3,2,1,0:T(8,128)(2,1)S(1)}) fusion(bf16[3,4,2,4,64,384]{5,4,3,2,1,0:T(8,128)(2,1)} %get-tuple-element.17), kind=kLoop, calls=%fused_computation.33 | loop fusion | bytes 9437184 | tf_op jit(solution)/shard_map/slice | solution.py:630
  107.8 0.7 fusion.10
  108.5 0.7 fusion.11
  109.2 0.0 copy-start.1
  109.2 0.0 copy-start.2
  109.3 0.0 copy-start.3
  109.3 0.9 multiply_convert_fusion.2
  110.1 0.1 pad_maximum_fusion.hid
  110.2 0.0 copy-done.1
  110.2 0.1 copy-done.2
  110.3 0.0 copy-done.3
  110.3 0.0 copy-start.5
  110.3 159.4 %shard_map.129 = (bf16[8,16,2048]{2,1,0:T(8,128)(2,1)S(1)}, f32[3,32,768]{2,1,0:T(8,128)S(1)}) custom-call(bf16[2,128,2048]{2,1,0:T(8,128)(2,1)S(1)} %bitcast.56, bf16[2,128,2048]{2,1,0:T(8,128)(2,1)S(1)} %bitcast.58, bf16[2,128,1024]{2,1,0:T(8,128)(2,1)S(1)} %bitcast.62, bf16[2,128,1024]{2,1,0:T(8,128)(2,1)S(1)} %bitcast.63, ...), custom_call_target="tpu_custom_call" | custom-call | tf_op jit(solution)/shard_map/pallas_call | solution.py:638
  269.7 0.0 copy-done.5
  269.7 0.9 convolution_convert_fusion
  270.6 1.1 fusion.3
  271.8 0.7 copy.27
  (4 shorter events, 0.1 us)
Async XLA Ops:
  0.6 5.2 %copy-start = (bf16[64,2048]{1,0:T(8,128)(2,1)S(1)}, bf16[64,2048]{1,0:T(8,128)(2,1)}, u32[]{:S(2)}) copy-start(bf16[64,2048]{1,0:T(8,128)(2,1)} %param.12) | copy-start | bytes 786436
  5.9 1.0 copy-start.4
  109.2 1.0 copy-start.1
  109.2 1.0 copy-start.2
  109.3 1.1 copy-start.3
  110.3 159.4 %copy-start.5 = (s32[128]{0:T(128)S(1)}, s32[128]{0:T(128)}, u32[]{:S(2)}) copy-start(s32[128]{0:T(128)} %param.13) | copy-start | bytes 1540

commit v3 on v2

--- a/solution.py
+++ b/solution.py
@@ -213,98 +213,6 @@
 
 
 GATHER_SEMS = 17
-
-
-EARLY = 4
-
-
-def dispatch_kernel(
-    tok, grd, wts, xt, xg, g, relay, xpt, xpg,
-    s_row, r_row, s_fwd, r_fwd, s_rl, r_rl, s_wt, r_wt, s_g, r_g, s_x, r_x, s_xf, r_xf,
-):
-    y, t, l, x, c = place()
-    other, across = {"c": 1 - c}, {"l": 1 - l}
-    greet(
-        [other] + gather_peers(),
-        [worker_of_rows(e) for e in range(8)]
-        + [source_of_rows(s) for s in range(8)]
-        + [worker_of_block(h) for h in range(2)]
-        + [sender_of_block(k) for k in range(2)]
-        + [relay_to(), relay_from()],
-    )
-    to_relay = (wts, relay, s_rl, r_rl, relay_to())
-    send_or_copy(*to_relay)
-    row_sends = []
-    slot = 2 * x + c
-    for src, dst, which in ((tok, xt, 0), (grd, xg, 1)):
-        for k, off in enumerate((4, 2, 6, 1, 7, 3, 5, 0)):
-            e = (t + off) % 8
-            row_sends.append(
-                (src.at[e], dst.at[l, slot], s_row.at[which, k], r_row.at[which, slot], worker_of_rows(e))
-            )
-    for a in row_sends[:EARLY]:
-        send_or_copy(*a)
-    landed(relay, r_rl)
-    chunk = g.at[:, y, t // 4, t % 4, pl.ds(pl.multiple_of(l * 32, 32), 32)]
-    weight_sends = [(relay.at[h], chunk, s_wt.at[h], r_wt.at[l], worker_of_block(h)) for h in range(2)]
-    for a in weight_sends:
-        send_or_copy(*a)
-    mine = g.at[:, y, l, row_x(x, t)]
-    for k in range(2):
-        landed(mine.at[:, pl.ds(32 * k, 32)], r_wt.at[k])
-    swap = gather_swap(g, s_g, r_g)
-    for a in row_sends[EARLY:8]:
-        send_or_copy(*a)
-    steps = gather_steps(g, swap, s_g, r_g)
-    for _ in range(3):
-        next(steps)
-    for a in row_sends[8:]:
-        send_or_copy(*a)
-    next(steps)
-    forwards, crossings = [], []
-
-    def rows_in(dst, far, which):
-        for s in range(8):
-            part = dst.at[c, s]
-            landed(part, r_row.at[which, s])
-            f = remote(part, part, s_fwd.at[which, s], r_fwd.at[which, s], other)
-            f.start()
-            forwards.append(f)
-        for n in range(4):
-            cols = pl.ds(pl.multiple_of(512 * n + (1 - l) * 256, 256), 256)
-            f = remote(
-                dst.at[c, :, :, cols],
-                far.at[c, :, :, pl.ds(256 * n, 256)],
-                s_x.at[which, n],
-                r_x.at[which, n],
-                across,
-            )
-            f.start()
-            crossings.append(f)
-
-    def crossed(far, which):
-        for n in range(4):
-            piece = far.at[c, :, :, pl.ds(256 * n, 256)]
-            landed(piece, r_x.at[which, n])
-            f = remote(piece, piece, s_xf.at[which, n], r_xf.at[which, n], other)
-            f.start()
-            forwards.append(f)
-
-    rows_in(xt, xpt, 0)
-    next(steps)
-    crossed(xpt, 0)
-    rows_in(xg, xpg, 1)
-    next(steps)
-    for a in [to_relay] + weight_sends + row_sends:
-        wait_sent(*a)
-    crossed(xpg, 1)
-    for f in forwards + crossings:
-        f.wait_send()
-    for dst, far, which in ((xt, xpt, 0), (xg, xpg, 1)):
-        for s in range(8):
-            landed(dst.at[1 - c, s], r_fwd.at[which, s])
-        for n in range(4):
-            landed(far.at[1 - c, :, :, pl.ds(256 * n, 256)], r_xf.at[which, n])
 
 
 PAIRS = [(i, k) for i in range(4) for k in range(i, 4)]
@@ -424,11 +332,13 @@
     return new_weights, new_first, new_second
 
 
-def tree_kernel(
-    xt, xg, xpt, xpg, hid, master, moment1, moment2,
+def step_kernel(
+    tok, grd, gate, up, down, moment1, moment2,
     ret, got,
+    xt, xg, wts, relay_w, g3,
     ft, fg, fh, fs, gram, lines, relay, own_state, v, r, rel, vy, ry, rely, comb, g, part, came, rounded, via,
     box_a, box_b, box_c, box_d,
+    s_row, r_row, s_fwd, r_fwd, s_rw, r_rw, s_wt, r_wt, s_g3, r_g3, s_x, r_x, s_xf, r_xf,
     own, s_h, r_h, s_rl, r_rl, s_st, r_st, sv, rv, sw, rw,
     s_a, r_a, s_b, r_b, s_c, r_c, s_d, r_d, s_g, r_g, s_o, r_o, s_p, r_p, s_y, r_y, s_z, r_z,
 ):
@@ -438,24 +348,15 @@
     column = [ring("y", k) for k in range(1, 4)]
     row_home = [{"t": 2 * q + l, "l": k} for q in range(4) for k in range(2)]
     row_from = [{"t": e, "l": t % 2} for e in range(8)]
-    row_via = [{"x": s // 2, "c": s % 2} for s in range(8)]
     mine = 2 * l
     theirs = 2 * (1 - l)
-    local = [pltpu.make_async_copy(hid, fh.at[:, pl.ds(mine, 2)], own.at[8])]
-    for k, (src, far, dst) in enumerate(((xt, xpt, ft), (xg, xpg, fg))):
-        for n in range(4):
-            cols = pl.ds(pl.multiple_of(512 * n + l * 256, 256), 256)
-            local.append(
-                pltpu.make_async_copy(
-                    src.at[:, :, cols], dst.at[pl.ds(mine, 2), :, pl.ds(256 * n, 256)], own.at[4 * k + n]
-                )
-            )
-        local.append(pltpu.make_async_copy(far, dst.at[pl.ds(theirs, 2)], own.at[9 + k]))
-    for f in local:
-        f.start()
+    for m, master in enumerate((gate, up, down)):
+        wts[m] = master[0].astype(jnp.bfloat16)
     greet(
-        quad + wide + column,
-        [worker_of_block(h) for h in range(2)]
+        wide + column,
+        [worker_of_rows(e) for e in range(8)]
+        + [source_of_rows(s) for s in range(8)]
+        + [worker_of_block(h) for h in range(2)]
         + [sender_of_block(k) for k in range(2)]
         + [block_of_owner(h) for h in range(2)]
         + [owner_of_block(k) for k in range(2)]
@@ -463,14 +364,109 @@
         + row_home
         + row_from,
     )
-    cross = remote(hid, fh.at[:, pl.ds(mine, 2)], s_h, r_h, across)
-    cross.start()
+    wts_relay = (wts, relay_w, s_rw, r_rw, relay_to())
+    send_or_copy(*wts_relay)
+    row_sends = []
+    slot = 2 * x + c
+    for src, dst, which in ((tok, xt, 0), (grd, xg, 1)):
+        for k, off in enumerate((4, 2, 6, 1, 7, 3, 5, 0)):
+            e = (t + off) % 8
+            row_sends.append(
+                (src.at[e], dst.at[l, slot], s_row.at[which, k], r_row.at[which, slot], worker_of_rows(e))
+            )
+    landed(relay_w, r_rw)
+    chunk = g3.at[:, y, t // 4, t % 4, pl.ds(pl.multiple_of(l * 32, 32), 32)]
+    weight_sends = [(relay_w.at[:, :, pl.ds(384 * h, 384)], chunk, s_wt.at[h], r_wt.at[l], worker_of_block(h)) for h in range(2)]
+    for a in weight_sends:
+        send_or_copy(*a)
+    own_chunk = g3.at[:, y, l, row_x(x, t)]
+    for k in range(2):
+        landed(own_chunk.at[:, pl.ds(32 * k, 32)], r_wt.at[k])
+    swap = gather_swap(g3, s_g3, r_g3)
+    for a in row_sends[:8]:
+        send_or_copy(*a)
+    steps = gather_steps(g3, swap, s_g3, r_g3)
+    for _ in range(3):
+        next(steps)
+    for a in row_sends[8:]:
+        send_or_copy(*a)
+    next(steps)
+    forwards, crossings = [], []
+
+    def rows_in(dst, far, which):
+        for s in range(8):
+            part = dst.at[c, s]
+            landed(part, r_row.at[which, s])
+            f = remote(part, part, s_fwd.at[which, s], r_fwd.at[which, s], other)
+            f.start()
+            forwards.append(f)
+        for n in range(4):
+            cols = pl.ds(pl.multiple_of(512 * n + (1 - l) * 256, 256), 256)
+            f = remote(
+                dst.at[c, :, :, cols],
+                far.at[mine + c, :, :, pl.ds(256 * n, 256)],
+                s_x.at[which, n],
+                r_x.at[which, n],
+                across,
+            )
+            f.start()
+            crossings.append(f)
+
+    def crossed(far, which):
+        for n in range(4):
+            piece = far.at[theirs + c, :, :, pl.ds(256 * n, 256)]
+            landed(piece, r_x.at[which, n])
+            f = remote(piece, piece, s_xf.at[which, n], r_xf.at[which, n], other)
+            f.start()
+            forwards.append(f)
+
+    rows_in(xt, ft, 0)
+    next(steps)
+    crossed(ft, 0)
+    rows_in(xg, fg, 1)
+    next(steps)
+    for a in [wts_relay] + weight_sends + row_sends:
+        wait_sent(*a)
+    crossed(fg, 1)
+    for f in forwards + crossings:
+        f.wait_send()
+    for dst, far, which in ((xt, ft, 0), (xg, fg, 1)):
+        for s in range(8):
+            landed(dst.at[1 - c, s], r_fwd.at[which, s])
+        for n in range(4):
+            landed(far.at[theirs + 1 - c, :, :, pl.ds(256 * n, 256)], r_xf.at[which, n])
+
+    local = []
+    for k, (src, dst) in enumerate(((xt, ft), (xg, fg))):
+        for n in range(4):
+            cols = pl.ds(pl.multiple_of(512 * n + l * 256, 256), 256)
+            local.append(
+                pltpu.make_async_copy(
+                    src.at[:, :, :, cols], dst.at[pl.ds(mine, 2), :, :, pl.ds(256 * n, 256)], own.at[4 * k + n]
+                )
+            )
+    for f in local:
+        f.start()
     to_relay = [
         (src, relay.at[k], s_rl.at[k], r_rl.at[k], relay_to())
-        for k, src in enumerate((master.at[0], moment1.at[0, 2], moment2.at[0, 2]))
+        for k, src in enumerate((down.at[0], moment1.at[0, 2], moment2.at[0, 2]))
     ]
     for a in to_relay:
         send_or_copy(*a)
+    rows_t, rows_g = xt[...].reshape(256, 2048), xg[...].reshape(256, 2048)
+    gate_pre = jnp.dot(rows_t, g3[0].reshape(2048, 384), preferred_element_type=jnp.float32)
+    up_pre = jnp.dot(rows_t, g3[1].reshape(2048, 384), preferred_element_type=jnp.float32)
+    back_hidden = jnp.dot(rows_g, g3[2].reshape(2048, 384), preferred_element_type=jnp.float32)
+    sigmoid_gate = jax.nn.sigmoid(gate_pre)
+    active_gate = gate_pre * sigmoid_gate
+    hidden = active_gate * up_pre
+    d_gate = back_hidden * up_pre * sigmoid_gate * (1.0 + gate_pre * (1.0 - sigmoid_gate))
+    d_up = back_hidden * active_gate
+    for m, value in enumerate((d_gate, d_up, hidden)):
+        fh[m, pl.ds(mine, 2)] = value.astype(jnp.bfloat16).reshape(2, 128, 384)
+    factors = fh.at[:, pl.ds(mine, 2)]
+    cross = remote(factors, factors, s_h, r_h, across)
+    cross.start()
     for f in local:
         f.wait()
     for k in range(3):
@@ -483,8 +479,8 @@
         send_or_copy(*a)
 
     for n, (i, k) in enumerate(PAIRS):
-        gram[0, n] = lax.dot_general(ft[i], ft[k], LAST, preferred_element_type=jnp.float32)
-        gram[1, n] = lax.dot_general(fg[i], fg[k], LAST, preferred_element_type=jnp.float32)
+        gram[0, n] = lax.dot_general(ft[i].reshape(128, 1024), ft[k].reshape(128, 1024), LAST, preferred_element_type=jnp.float32)
+        gram[1, n] = lax.dot_general(fg[i].reshape(128, 1024), fg[k].reshape(128, 1024), LAST, preferred_element_type=jnp.float32)
     landed(fh.at[:, pl.ds(theirs, 2)], r_h)
     lines[...] = jnp.zeros_like(lines)
     for n, (i, k) in enumerate(PAIRS):
@@ -498,7 +494,7 @@
             fs[m, pl.ds(128 * k, 128), :] = (fh[m, k].astype(jnp.float32) * w).astype(jnp.bfloat16)
     for src, matrices in ((ft, (0, 1)), (fg, (2,))):
         for n in range(4):
-            cols = src[:, :, pl.ds(256 * n, 256)].reshape(512, 256)
+            cols = src[:, :, :, pl.ds(256 * n, 256)].reshape(512, 256)
             for m in matrices:
                 block = lax.dot_general(
                     cols, fs[m], (((0,), (0,)), ((), ())), preferred_element_type=jnp.float32
@@ -542,24 +538,27 @@
         for k in range(2):
             block = lax.dot_general(fh[2, mine + k], rows, LAST, preferred_element_type=jnp.float32)
             part[k, :, :, pl.ds(256 * n, 256)] = block.reshape(8, 16, 256)
-    swaps = []
-    for s in range(8):
+    swaps, backs = [], []
+    turn = 2 * tree_place(x, t)
+    order = [(turn + k) % 8 for k in range(8)]
+    for s in order:
         f = remote(part.at[1 - c, s], came.at[s], s_p.at[s], r_p.at[s], other)
         f.start()
         swaps.append(f)
-    backs = []
-    slot = 2 * tree_place(x, t) + c
-    for s in range(8):
+    for s in order:
         landed(came.at[s], r_p.at[s])
         rounded[s] = (part[c, s] + came[s]).astype(jnp.bfloat16)
-        a = (rounded.at[s], via.at[slot], s_y.at[s], r_y.at[slot], row_via[s])
+        a = (rounded.at[s], via.at[turn + c], s_y.at[s], r_y.at[turn + c], {"x": s // 2, "c": s % 2})
         send_or_copy(*a)
         backs.append(a)
-    for q in range(8):
-        landed(via.at[q], r_y.at[q])
-        a = (via.at[q], ret.at[t], s_z.at[q], r_z.at[t], row_home[q])
-        send_or_copy(*a)
-        backs.append(a)
+    for k in range(4):
+        q = (x + 4 - k) % 4
+        for n in range(2):
+            at = 2 * q + n
+            landed(via.at[at], r_y.at[at])
+            a = (via.at[at], ret.at[t], s_z.at[at], r_z.at[t], {"t": 2 * q + l, "l": n})
+            send_or_copy(*a)
+            backs.append(a)
     cross.wait_send()
     for f in swaps:
         f.wait_send()
@@ -606,43 +605,20 @@
     sent_tokens = jnp.where(live_slots[:, None], jnp.take(tokens, route, axis=0), 0)
     sent_grads = jnp.where(live_slots[:, None], jnp.take(cotangent, route, axis=0), 0)
     masters = jnp.stack([gate_master[0], up_master[0], down_master[0]])
-    halves = jnp.moveaxis(masters.astype(bf16).reshape(3, 32, 2, 384), 2, 0)
-    xt, xg, weights, _, xpt, xpg = call(
-        dispatch_kernel,
-        (
-            shape((2, 8, 16, 2048)),
-            shape((2, 8, 16, 2048)),
-            shape((3, 4, 2, 4, 64, 384)),
-            shape((2, 3, 32, 384)),
-            shape((2, 8, 16, 1024)),
-            shape((2, 8, 16, 1024)),
-        ),
-        [ANY] * 3,
-        [ANY] * 6,
-        [DMA((2, 8))] * 4 + [DMA(())] * 2 + [DMA((2,))] * 2 + [DMA((GATHER_SEMS,))] * 2 + [DMA((2, 4))] * 4,
-        0,
-    )(sent_tokens.reshape(8, 16, 2048), sent_grads.reshape(8, 16, 2048), halves)
-    xt = xt.reshape(256, 2048)
-    xg = xg.reshape(256, 2048)
-    weights = weights.reshape(3, 2048, 384)
-    gate_pre = jnp.dot(xt, weights[0], preferred_element_type=f32)
-    up_pre = jnp.dot(xt, weights[1], preferred_element_type=f32)
-    back_hidden = jnp.dot(xg, weights[2], preferred_element_type=f32)
-    sigmoid_gate = jax.nn.sigmoid(gate_pre)
-    active_gate = gate_pre * sigmoid_gate
-    hidden = (active_gate * up_pre).astype(bf16)
-    d_gate = (back_hidden * up_pre * sigmoid_gate * (1.0 + gate_pre * (1.0 - sigmoid_gate))).astype(bf16)
-    d_up = (back_hidden * active_gate).astype(bf16)
-    factors = jnp.stack([d_gate, d_up, hidden]).reshape(3, 2, 128, 384)
     box = pltpu.VMEM((16, 32, 128), f32)
     returned, combined = call(
-        tree_kernel,
+        step_kernel,
         (shape((8, 16, 2048)), shape((3, 32, 768), f32)),
-        [ANY] * 8,
+        [ANY] * 2 + [VMEM] * 3 + [ANY] * 2,
         [ANY] * 2,
         [
-            pltpu.VMEM((4, 128, 1024), bf16),
-            pltpu.VMEM((4, 128, 1024), bf16),
+            pltpu.VMEM((2, 8, 16, 2048), bf16),
+            pltpu.VMEM((2, 8, 16, 2048), bf16),
+            pltpu.VMEM((3, 32, 768), bf16),
+            pltpu.VMEM((3, 32, 768), bf16),
+            pltpu.VMEM((3, 4, 2, 4, 64, 384), bf16),
+            pltpu.VMEM((4, 8, 16, 1024), bf16),
+            pltpu.VMEM((4, 8, 16, 1024), bf16),
             pltpu.VMEM((3, 4, 128, 384), bf16),
             pltpu.VMEM((3, 512, 384), bf16),
             pltpu.VMEM((2, 10, 128, 128), f32),
@@ -665,8 +641,13 @@
             box,
             box,
             pltpu.VMEM((4, 32, 128), f32),
-            DMA((11,)),
         ]
+        + [DMA((2, 8))] * 4
+        + [DMA(())] * 2
+        + [DMA((2,))] * 2
+        + [DMA((GATHER_SEMS,))] * 2
+        + [DMA((2, 4))] * 4
+        + [DMA((8,))]
         + [DMA(())] * 2
         + [DMA((3,))] * 2
         + [DMA((2,))] * 2
@@ -679,11 +660,10 @@
         + [DMA((8,))] * 6,
         1,
     )(
-        xt.reshape(2, 128, 2048),
-        xg.reshape(2, 128, 2048),
-        xpt.reshape(2, 128, 1024),
-        xpg.reshape(2, 128, 1024),
-        factors,
+        sent_tokens.reshape(8, 16, 2048),
+        sent_grads.reshape(8, 16, 2048),
+        gate_master,
+        up_master,
         down_master,
         first_moment,
         second_moment,

time: 273 us -> 254 us (0.930)
  the two profiles are of different devices: /device:TPU:33 before, /device:TPU:7 now
where the time goes in v3:
time: 254 us; the launch traced here: 253 us
  Pallas kernels  245 us (96%)
  local copies, waits for them, and re-layouts  4.92 us (2%)
    pallas_call x1, Pallas kernels, shards(): call(step_kernel, (shape((8, 16, 2048)), shape((3, 32, 768), f32)), [ANY]...  245 us

profile of v3, /device:TPU:7, one launch (start us, length us, event | category | flops | bytes accessed | tf_op | source)
XLA Modules:
  0.0 252.7 jit_solution(11218306113560030724)
XLA Ops:
  0.6 0.0 copy-start
  0.6 0.0 copy-start.8
  0.7 0.7 copy-done.8
  1.3 0.1 broadcast_in_dim.45
  1.4 0.0 copy-start.7
  1.4 0.1 reshape.60
  1.5 0.6 copy-done.7
  2.1 0.0 copy-done
  2.1 0.0 copy-start.6
  2.1 0.9 gather_fusion
  3.1 0.0 copy-done.6
  3.1 0.9 gather_fusion.1
  4.0 0.0 copy-start.1
  4.0 0.0 copy-start.2
  4.0 0.0 copy-start.3
  4.0 0.0 copy-start.4
  4.1 0.0 copy-start.5
  4.1 0.2 select_select_fusion
  4.3 0.7 copy-done.1
  5.0 0.1 copy-done.2
  5.1 0.0 copy-done.3
  5.1 0.0 copy-done.4
  5.1 0.0 copy-done.5
  5.1 244.8 %shard_map.128 = (bf16[8,16,2048]{2,1,0:T(8,128)(2,1)S(1)}, f32[3,32,768]{2,1,0:T(8,128)S(1)}) custom-call(bf16[8,16,2048]{2,1,0:T(8,128)(2,1)S(1)} %bitcast.25, bf16[8,16,2048]{2,1,0:T(8,128)(2,1)S(1)} %bitcast.24, f32[1,32,768]{2,1,0:T(8,128)S(1)} %copy-done.3, f32[1,32,768]{2,1,0:T(8,128)S(1)} %copy-done.4, f32[1,32,768]{2,1,0:T(8,128)S(1)} %copy-done.5, ...), custom_call_target="tpu_custom_call" | custom-call | tf_op jit(solution)/shard_map/pallas_call | solution.py:609
  250.0 1.1 fusion.2
  251.1 0.9 convolution_convert_fusion
  252.0 0.7 copy.17
  (6 shorter events, 0.0 us)
Async XLA Ops:
  0.6 1.5 copy-start
  0.6 0.7 copy-start.8
  1.4 0.7 copy-start.7
  2.1 1.0 copy-start.6
  4.0 1.0 copy-start.1
  4.0 1.0 copy-start.2
  4.0 1.1 copy-start.3
  4.0 1.1 copy-start.4
  4.1 1.1 copy-start.5
